TPU v7x, 32 devices: a whole 2x2x4 slice. The times are simulated.
32 devices in a mesh: dp: 4 (over x, core), expert: 8 (over z, y).
Axes of the slice: x: 2, y: 2, z: 4, core: 2. Of those that a mesh axis runs over, the one named last changes fastest.
Arguments:
- tokens: bfloat16 [2048, 4096], P('expert'), may hold values from -6 to 6
- expert_ids: int32 [2048, 8], P('expert'), may hold values from 0 to 255, as said below
- combine_weight: float32 [2048, 8], P('expert'), may hold values from 0.1 to 1
- old_plan: int32 [8], replicated, may hold values from 0 to 255, as said below
- new_plan: int32 [8], replicated, may hold values from 0 to 255, as said below
- gate_weight: bfloat16 [8, 4096, 2048], P('expert', None, 'dp'), may hold values from -0.09375 to 0.09375
- up_weight: bfloat16 [8, 4096, 2048], P('expert', None, 'dp'), may hold values from -0.09375 to 0.09375
- down_weight: bfloat16 [8, 2048, 4096], P('expert', 'dp'), may hold values from -0.125 to 0.125
- shared_gate: bfloat16 [4096, 2048], P(None, 'dp'), may hold values from -0.09375 to 0.09375
- shared_up: bfloat16 [4096, 2048], P(None, 'dp'), may hold values from -0.09375 to 0.09375
- shared_down: bfloat16 [2048, 4096], P('dp'), may hold values from -0.125 to 0.125
Outputs:
- mixed_out: bfloat16 [2048, 4096], P('expert', 'dp')
Inputs may be any that keep to these rules, and one draw needn't show every extreme that they name: `old_plan`: the 8 experts are different. `new_plan`: slot s holds old_plan[s] or old_plan[s - 1] (slot 0 may take from slot 7); slots 0, 4 and 7 change; apart from slots 0 and 7, two neighbouring slots never both change. `expert_ids`: the 8 experts of a token are different; the tokens of one device send at most 2 kept routes to the slots of one expert together, and some slot gets exactly 2 from the tokens of every device.
All inputs are finite; a program needn't handle non-finite values.
Results may differ from a plain program's by a relative error of at most 0.014.
Values may be sent and summed in bfloat16 or wider, within the bound.
No kernel may reach another device: no remote copies, remote signals or barrier semaphores. Data moves between devices by JAX's collectives and lax.ppermute only.
A program may use at most 64 MiB of HBM per device.

v0:
```python
import jax
import jax.numpy as jnp
from jax import lax
from jax.sharding import PartitionSpec as P

CAP = 2


def route_slots(expert_ids, token_index, new_plan):
    matches = (expert_ids[:, :, None] == new_plan[None, None, :]).astype(jnp.int32)
    counted = jnp.sum(matches, axis=2, keepdims=True)
    before = jnp.cumsum(matches, axis=2) - matches
    wanted = jnp.remainder(token_index[:, None, None], jnp.maximum(counted, 1))
    return matches * (before == wanted).astype(jnp.int32)


def expert_block(row_block, gate_part, up_part, down_part):
    gate_value = jnp.dot(row_block, gate_part, preferred_element_type=jnp.float32)
    up_value = jnp.dot(row_block, up_part, preferred_element_type=jnp.float32)
    hidden = (jax.nn.silu(gate_value) * up_value).astype(jnp.bfloat16)
    return jnp.dot(hidden, down_part, preferred_element_type=jnp.float32).astype(jnp.bfloat16)


def combine_routes(rows, row_index, route_scale):
    total = jnp.zeros((row_index.shape[0], rows.shape[1]), jnp.float32)
    for route in range(row_index.shape[1]):
        picked = rows[row_index[:, route]].astype(jnp.float32)
        total = total + route_scale[:, route][:, None] * picked
    return total


def local(
    tokens,
    expert_ids,
    combine_weight,
    old_plan,
    new_plan,
    gate_weight,
    up_weight,
    down_weight,
    shared_gate,
    shared_up,
    shared_down,
):
    slot_count = lax.axis_size("expert")
    own_index = lax.axis_index("expert")
    tok_rows = tokens.shape[0]
    route_count = expert_ids.shape[1]
    model_width = tokens.shape[1]
    token_index = own_index * tok_rows + jnp.arange(tok_rows, dtype=jnp.int32)
    chosen = route_slots(expert_ids, token_index, new_plan)
    changed = (new_plan != old_plan).astype(jnp.int32)
    gate_now = gate_weight[0]
    up_now = up_weight[0]
    down_now = down_weight[0]
    staying = chosen * (1 - changed)[None, None, :]
    targets = staying + jnp.roll(chosen * changed[None, None, :], -1, axis=2)
    capacity = 2 * CAP
    flat_targets = targets.reshape(tok_rows * route_count, slot_count)
    earlier = jnp.cumsum(flat_targets, axis=0) - flat_targets
    position = jnp.sum(earlier * flat_targets, axis=1).reshape(tok_rows, route_count)
    columns = lax.broadcasted_iota(jnp.int32, (1, 1, 1, capacity), 3)
    placed = targets[:, :, :, None] * (position[:, :, None, None] == columns).astype(jnp.int32)
    routing = jnp.sum(placed, axis=1).reshape(tok_rows, slot_count * capacity)
    slot_numbers = lax.broadcasted_iota(jnp.int32, (1, 1, slot_count), 2)
    slot_of = jnp.sum(targets * slot_numbers, axis=2)
    kept = jnp.sum(targets, axis=2)
    row_index = slot_of * capacity + position * kept
    route_scale = combine_weight * kept.astype(jnp.float32)
    outgoing = lax.dot_general(
        routing.astype(jnp.bfloat16),
        tokens,
        (((0,), (0,)), ((), ())),
        preferred_element_type=jnp.float32,
    )
    outgoing = outgoing.astype(jnp.bfloat16).reshape(slot_count, capacity, model_width)
    arrived = lax.all_to_all(outgoing, "expert", split_axis=0, concat_axis=0, tiled=True)
    senders, item_count, features = arrived.shape
    result = expert_block(
        arrived.reshape(senders * item_count, features), gate_now, up_now, down_now
    )
    slot_part = result.reshape(senders, item_count, features)
    shared_part = expert_block(tokens, shared_gate, shared_up, shared_down)
    slot_rows = slot_part.reshape(slot_count * capacity, model_width).astype(jnp.float32)
    slot_sum, shared_sum = (
        lax.psum_scatter(
            slot_rows.astype(jnp.bfloat16), "dp", scatter_dimension=1, tiled=True
        ).astype(jnp.float32),
        lax.psum_scatter(
            shared_part.astype(jnp.float32).astype(jnp.bfloat16),
            "dp",
            scatter_dimension=1,
            tiled=True,
        ).astype(jnp.float32),
    )
    returned = lax.all_to_all(
        slot_sum.reshape(slot_count, capacity, slot_sum.shape[1]).astype(jnp.bfloat16),
        "expert",
        split_axis=0,
        concat_axis=0,
        tiled=True,
    ).astype(jnp.float32)
    routed = combine_routes(
        returned.reshape(slot_count * capacity, returned.shape[2]), row_index, route_scale
    )
    mixed_out = (shared_sum + routed).astype(jnp.bfloat16)
    return mixed_out


def solution(mesh):
    in_specs = (
        P("expert", None),
        P("expert", None),
        P("expert", None),
        P(),
        P(),
        P("expert", None, "dp"),
        P("expert", None, "dp"),
        P("expert", "dp", None),
        P(None, "dp"),
        P(None, "dp"),
        P("dp", None),
    )
    out_specs = P("expert", "dp")
    return jax.shard_map(local, mesh=mesh, in_specs=in_specs, out_specs=out_specs, check_vma=False)
```

profile of v0, /device:TPU:0, one launch (start us, length us, event | category | flops | bytes accessed | tf_op | source)
XLA Modules:
  0.0 109.8 jit_solution(14721196537238567470)
XLA Ops:
  6.5 0.0 copy-start
  6.5 0.0 copy-start.2
  6.5 0.0 copy-start.1
  6.5 0.9 convert_reduce_fusion
  7.5 0.8 compare_convert_fusion
  8.3 0.7 broadcast_subtract_fusion
  8.9 0.1 broadcast_maximum_fusion
  9.1 0.1 reduce_window_sum.28
  9.1 0.8 fusion.20
  10.0 0.8 copy.43
  10.8 0.3 copy.42
  11.1 0.1 copy.47
  11.3 0.1 concatenate.17
  11.4 0.1 copy.45
  11.5 0.1 max.19
  11.7 0.1 rem.22.clone
  11.8 0.1 rem.24
  11.9 0.1 eq.81
  12.0 1.2 %copy.46 = s32[256,8,7]{1,0,2:T(8,128)} copy(s32[256,8,7]{0,2,1:T(8,128)S(1)} %slice.98) | data formatting | bytes 114688 | tf_op jit(solution)/shard_map/jit(_roll_static)/slice | solution.py:57
  13.2 1.6 %concatenate.16 = s32[2048,7]{0,1:T(8,128)S(1)} reshape(s32[256,8,7]{1,0,2:T(8,128)} %copy.46) | data formatting | bytes 114688 | tf_op jit(solution)/shard_map/jit(_roll_static)/concatenate | solution.py:57
  14.9 0.5 reduce_window_sum.29
  15.4 0.0 copy-done.2
  15.4 0.0 copy-done.1
  15.4 0.1 multiply_reduce_fusion.1
  15.5 0.1 add_select_fusion
  15.6 0.1 fusion.38
  15.8 2.3 %reduce-window.6 = s32[8,16,128]{2,1,0:T(8,128)S(1)} reduce-window(s32[8,16,128]{2,1,0:T(8,128)S(1)} %copy.48, s32[]{:T(128)} %constant.15.clone.1), window={size=1x1x128 pad=0_0x0_0x127_0}, to_apply=%region_4.5 | reduce-window | flops 2080768 | bytes 131076 | tf_op jit(solution)/shard_map/reduce-window
  18.0 0.3 slice_reduce_fusion
  18.3 0.2 reduce-window.9
  18.5 0.1 add_bitcast_fusion
  18.6 0.1 fusion.27
  18.7 0.1 eq.88
  18.8 0.1 copy.49
  19.0 0.0 copy-done
  19.0 0.5 convolution_convert_fusion.2
  19.5 0.8 reshape.117
  20.3 7.3 %all-to-all-start = ((bf16[8,4,4096]{2,1,0:T(4,128)(2,1)}), bf16[8,4,4096]{2,1,0:T(4,128)(2,1)S(1)}, u32[]{:S(2)}, u32[]{:S(2)}) async-start(bf16[8,4,4096]{2,1,0:T(4,128)(2,1)} %reshape.117), calls=%async_computation.1 | async-start | bytes 524288 | tf_op jit(solution)/shard_map/all_to_all | solution.py:77
  27.6 0.0 reduce-scatter.5.cloned.1.call-start
  27.6 3.4 %fusion.42 = f32[256,512]{1,0:T(8,128)S(1)} fusion(bf16[256,4096]{1,0:T(8,128)(2,1)S(1)} %copy-done, bf16[4096,512]{1,0:T(8,128)(2,1)} %param.19), kind=kOutput, calls=%fused_computation.88 | convolution fusion | flops 1073741824 | bytes 6815744 | tf_op jit(solution)/shard_map/dot_general | solution.py:18
  31.1 5.4 %all-to-all-done = bf16[8,4,4096]{2,1,0:T(4,128)(2,1)S(1)} async-done(((bf16[8,4,4096]{2,1,0:T(4,128)(2,1)}), bf16[8,4,4096]{2,1,0:T(4,128)(2,1)S(1)}, u32[]{:S(2)}, u32[]{:S(2)}) %all-to-all-start) | async-done | bytes 262176 | tf_op jit(solution)/shard_map/all_to_all | solution.py:77
  36.5 0.1 reshape.118
  36.6 3.0 %fusion.3 = f32[32,512]{1,0:T(8,128)S(1)} fusion(bf16[32,4096]{1,0:T(8,128)(2,1)S(1)} %reshape.118, bf16[1,4096,512]{2,1,0:T(8,128)(2,1)} %param.16), kind=kOutput, calls=%fused_computation.14 | convolution fusion | flops 134217728 | bytes 4521984 | tf_op jit(solution)/shard_map/dot_general | solution.py:18
  39.6 5.8 %convolution_convert_fusion.1 = bf16[32,4096]{1,0:T(8,128)(2,1)} fusion(bf16[1,512,4096]{2,1,0:T(8,128)(2,1)} %param.18, bf16[32,4096]{1,0:T(8,128)(2,1)S(1)} %reshape.118, bf16[1,4096,512]{2,1,0:T(8,128)(2,1)} %param.17, f32[32,512]{1,0:T(8,128)S(1)} %fusion.3), kind=kOutput, calls=%fused_computation.9 | convolution fusion | flops 268664832 | bytes 8978432 | tf_op jit(solution)/shard_map/dot_general | solution.py:21
  45.4 0.0 reduce-scatter.5.cloned.1.call-update
  45.4 0.0 copy-start.3
  45.4 0.0 reduce-scatter.3.cloned.1.call-start
  45.5 7.3 %convolution_convert_fusion = bf16[256,4096]{1,0:T(8,128)(2,1)} fusion(bf16[512,4096]{1,0:T(8,128)(2,1)} %param.21, bf16[256,4096]{1,0:T(8,128)(2,1)S(1)} %copy-done, bf16[4096,512]{1,0:T(8,128)(2,1)} %param.20, f32[256,512]{1,0:T(8,128)S(1)} %fusion.42), kind=kOutput, calls=%fused_computation.8 | convolution fusion | flops 2149318656 | bytes 13107200 | tf_op jit(solution)/shard_map/dot_general | solution.py:21
  52.7 0.0 reduce-scatter.3.cloned.1.call-update
  52.9 0.0 copy-done.3
  52.9 11.7 %reduce-scatter.5.cloned.1.call-done = bf16[32,1024]{1,0:T(8,128)(2,1)} async-done(((bf16[32,4096]{1,0:T(8,128)(2,1)}), bf16[32,1024]{1,0:T(8,128)(2,1)}) %reduce-scatter.5.cloned.1.call-update) | async-done | bytes 65552 | tf_op jit(solution)/shard_map/reduce_scatter | solution.py:86
  64.6 1.5 %convert_element_type.75 = bf16[8,4,1024]{2,1,0:T(4,128)(2,1)} reshape(bf16[32,1024]{1,0:T(8,128)(2,1)} %reduce-scatter.5.cloned.1.call-done) | data formatting | bytes 131072 | tf_op jit(solution)/shard_map/convert_element_type | solution.py:97
  66.1 5.5 %all-to-all-start.1 = ((bf16[8,4,1024]{2,1,0:T(4,128)(2,1)}), bf16[8,4,1024]{2,1,0:T(4,128)(2,1)S(1)}, u32[]{:S(2)}, u32[]{:S(2)}) async-start(bf16[8,4,1024]{2,1,0:T(4,128)(2,1)} %convert_element_type.75), calls=%async_computation.3 | async-start | bytes 131072 | tf_op jit(solution)/shard_map/all_to_all | solution.py:96
  71.6 6.9 %all-to-all-done.1 = bf16[8,4,1024]{2,1,0:T(4,128)(2,1)S(1)} async-done(((bf16[8,4,1024]{2,1,0:T(4,128)(2,1)}), bf16[8,4,1024]{2,1,0:T(4,128)(2,1)S(1)}, u32[]{:S(2)}, u32[]{:S(2)}) %all-to-all-start.1) | async-done | bytes 65568 | tf_op jit(solution)/shard_map/all_to_all | solution.py:96
  78.5 1.1 gather_fusion.7
  79.6 2.0 %gather_fusion.6 = f32[256,1024]{1,0:T(8,128)} fusion(f32[32,1024]{1,0:T(8,128)S(1)} %reshape.122, s32[1024]{0:T(1024)S(1)} %pad_clamp_fusion.1), kind=kCustom, calls=%fused_computation.6 | custom fusion | bytes 2098176 | tf_op jit(solution)/shard_map/gather | solution.py:27
  81.6 2.0 %gather_fusion.5 = f32[256,1024]{1,0:T(8,128)} fusion(f32[32,1024]{1,0:T(8,128)S(1)} %reshape.122, s32[1024]{0:T(1024)S(1)} %pad_clamp_fusion.2), kind=kCustom, calls=%fused_computation.5 | custom fusion | bytes 2098176 | tf_op jit(solution)/shard_map/gather | solution.py:27
  83.7 2.0 %gather_fusion.4 = f32[256,1024]{1,0:T(8,128)} fusion(f32[32,1024]{1,0:T(8,128)S(1)} %reshape.122, s32[1024]{0:T(1024)S(1)} %pad_clamp_fusion.3), kind=kCustom, calls=%fused_computation.4 | custom fusion | bytes 2098176 | tf_op jit(solution)/shard_map/gather | solution.py:27
  85.7 2.1 %gather_fusion.3 = f32[256,1024]{1,0:T(8,128)} fusion(f32[32,1024]{1,0:T(8,128)S(1)} %reshape.122, s32[1024]{0:T(1024)S(1)} %pad_clamp_fusion.4), kind=kCustom, calls=%fused_computation.3 | custom fusion | bytes 2098176 | tf_op jit(solution)/shard_map/gather | solution.py:27
  87.7 2.0 %gather_fusion.2 = f32[256,1024]{1,0:T(8,128)} fusion(f32[32,1024]{1,0:T(8,128)S(1)} %reshape.122, s32[1024]{0:T(1024)S(1)} %pad_clamp_fusion.5), kind=kCustom, calls=%fused_computation.2 | custom fusion | bytes 2098176 | tf_op jit(solution)/shard_map/gather | solution.py:27
  89.8 2.0 %gather_fusion.1 = f32[256,1024]{1,0:T(8,128)} fusion(f32[32,1024]{1,0:T(8,128)S(1)} %reshape.122, s32[1024]{0:T(1024)S(1)} %pad_clamp_fusion.6), kind=kCustom, calls=%fused_computation.1 | custom fusion | bytes 2098176 | tf_op jit(solution)/shard_map/gather | solution.py:27
  91.8 2.1 %gather_fusion = f32[256,1024]{1,0:T(8,128)} fusion(f32[32,1024]{1,0:T(8,128)S(1)} %reshape.122, s32[1024]{0:T(1024)S(1)} %pad_clamp_fusion.7), kind=kCustom, calls=%fused_computation | custom fusion | bytes 2098176 | tf_op jit(solution)/shard_map/gather | solution.py:27
  93.9 4.4 %reduce-scatter.3.cloned.1.call-done = bf16[256,1024]{1,0:T(8,128)(2,1)} async-done(((bf16[256,4096]{1,0:T(8,128)(2,1)}), bf16[256,1024]{1,0:T(8,128)(2,1)}) %reduce-scatter.3.cloned.1.call-update) | async-done | bytes 524304 | tf_op jit(solution)/shard_map/reduce_scatter | solution.py:89
  98.3 4.7 %add_convert_fusion = bf16[256,1024]{1,0:T(8,128)(2,1)} fusion(f32[256,1024]{1,0:T(8,128)S(1)} %gather_fusion.7, f32[256,1024]{1,0:T(8,128)} %gather_fusion.6, f32[256,1024]{1,0:T(8,128)} %gather_fusion.5, f32[256,1024]{1,0:T(8,128)} %gather_fusion.4, f32[256,1024]{1,0:T(8,128)} %gather_fusion.3, f32[256,1024]{1,0:T(8,128)} %gather_fusion.2, ...), kind=kLoop, calls=%fused_computation.20 | loop fusion | flops 4718592 | bytes 9445376 | tf_op jit(solution)/shard_map/convert_element_type | solution.py:106
  (22 shorter events, 0.2 us)
Async XLA Ops:
  6.5 12.4 %copy-start = (bf16[256,4096]{1,0:T(8,128)(2,1)S(1)}, bf16[256,4096]{1,0:T(8,128)(2,1)}, u32[]{:S(2)}) copy-start(bf16[256,4096]{1,0:T(8,128)(2,1)} %param.11) | copy-start | bytes 6291460
  6.5 8.8 %copy-start.2 = (s32[8]{0:T(128)S(1)}, s32[8]{0:T(128)}, u32[]{:S(2)}) copy-start(s32[8]{0:T(128)} %param.15) | copy-start | bytes 100
  6.5 8.8 %copy-start.1 = (s32[256,8]{0,1:T(8,128)S(1)}, s32[256,8]{0,1:T(8,128)}, u32[]{:S(2)}) copy-start(s32[256,8]{0,1:T(8,128)} %param.12) | copy-start | bytes 24580
  20.3 16.2 %all-to-all-start = ((bf16[8,4,4096]{2,1,0:T(4,128)(2,1)}), bf16[8,4,4096]{2,1,0:T(4,128)(2,1)S(1)}, u32[]{:S(2)}, u32[]{:S(2)}) async-start(bf16[8,4,4096]{2,1,0:T(4,128)(2,1)} %reshape.117), calls=%async_computation.1 | async-start | bytes 524288 | tf_op jit(solution)/shard_map/all_to_all | solution.py:77
  27.6 37.0 %reduce-scatter.5.cloned.1.call-start = ((), (), s32[]{:S(2)}) async-start(), calls=%async_computation.5 | async-start | bytes 327680 | tf_op jit(solution)/shard_map/reduce_scatter | solution.py:86
  45.4 7.5 %copy-start.3 = (f32[256,8]{0,1:T(8,128)S(1)}, f32[256,8]{0,1:T(8,128)}, u32[]{:S(2)}) copy-start(f32[256,8]{0,1:T(8,128)} %param.13) | copy-start | bytes 24580
  45.4 52.9 %reduce-scatter.3.cloned.1.call-start = ((), (), s32[]{:S(2)}) async-start(), calls=%async_computation.4 | async-start | bytes 2621440 | tf_op jit(solution)/shard_map/reduce_scatter | solution.py:89
  66.1 12.4 %all-to-all-start.1 = ((bf16[8,4,1024]{2,1,0:T(4,128)(2,1)}), bf16[8,4,1024]{2,1,0:T(4,128)(2,1)S(1)}, u32[]{:S(2)}, u32[]{:S(2)}) async-start(bf16[8,4,1024]{2,1,0:T(4,128)(2,1)} %convert_element_type.75), calls=%async_computation.3 | async-start | bytes 131072 | tf_op jit(solution)/shard_map/all_to_all | solution.py:96
Sparse Core Ops, SparseCore 0:
  45.5 19.0 reduce-scatter.4
  67.1 31.1 reduce-scatter.2
where the time goes:
time: 110 us
  waiting for transfers between devices  28.4 us (26%)
  local copies, waits for them, and re-layouts  23.7 us (22%)
  matrix products  20 us (18%)
  between operations  13.7 us (12%)
  starting transfers between devices  12.9 us (12%)
  other arithmetic  11.2 us (10%)
    gather x8, local copies, waits for them, and re-layouts, combine_routes(): picked = rows[row_index[:, route]].astype(jnp.float32)  15.4 us
    dot_general x2, matrix products, expert_block(): jnp.dot(hidden, down_part, preferred_element_type=jnp.float32)  13.1 us
    reduce_scatter x1, waiting for transfers between devices, local(): lax.psum_scatter(slot_rows.astype(jnp.bfloat16), 'dp', scatter_dimension=...  11.7 us
    all_to_all x1, starting transfers between devices, local(): lax.all_to_all(outgoing, 'expert', split_axis=0, concat_axis=0, tiled=True)  7.31 us
    all_to_all x1, waiting for transfers between devices, local(): lax.all_to_all(slot_sum.reshape(slot_count, capacity, slot_sum.shape[1])....  6.88 us
    dot_general x2, matrix products, expert_block(): jnp.dot(row_block, gate_part, preferred_element_type=jnp.float32)  6.42 us
    all_to_all x1, starting transfers between devices, local(): lax.all_to_all(slot_sum.reshape(slot_count, capacity, slot_sum.shape[1])....  5.52 us
    all_to_all x1, waiting for transfers between devices, local(): lax.all_to_all(outgoing, 'expert', split_axis=0, concat_axis=0, tiled=True)  5.44 us
  transfers between devices with their start and end apart: 4, of which 4 were waited for; matrix products, arithmetic and copies ran while one was open for 25% of the time, Pallas kernels for 0%

commit v1 on v0

v1 whole, which is shorter than its diff:
```python
import functools

import jax
import jax.numpy as jnp
from jax import lax
from jax.experimental import pallas as pl
from jax.experimental.pallas import tpu as pltpu
from jax.sharding import PartitionSpec as P

CAP = 2
BF = jnp.bfloat16
F32 = jnp.float32
VMEM = pltpu.VMEM
ANY = pl.ANY
SMEM = pltpu.SMEM


def silu_mul(gate_value, up_value):
    return (gate_value / (1.0 + jnp.exp(-gate_value)) * up_value).astype(BF)


def dot(a, b):
    return jnp.dot(a, b, preferred_element_type=F32)


def route_rows(ids, weight, old_ref, new_ref, rows, slots, slot_of_row, rank_of_row):
    tok = ids.shape[1]
    plan = jnp.full((rows, 1), -1, jnp.int32)
    for slot in range(slots):
        expert = old_ref[slot]
        after = (slot + 1) % slots
        present = (new_ref[slot] == expert) | (new_ref[after] == expert)
        plan = jnp.where(slot_of_row == slot, jnp.where(present, expert, -1), plan)
    hit = jnp.zeros((rows, tok), F32)
    scale = jnp.zeros((rows, tok), F32)
    for k in range(ids.shape[0]):
        same = ids[k : k + 1, :] == plan
        hit = jnp.where(same, 1.0, hit)
        if weight is not None:
            scale = jnp.where(same, weight[k : k + 1, :], scale)
    earlier = lax.broadcasted_iota(jnp.int32, (tok, tok), 0)
    later = lax.broadcasted_iota(jnp.int32, (tok, tok), 1)
    before = dot(hit.astype(BF), jnp.where(earlier < later, 1.0, 0.0).astype(BF))
    chosen = jnp.where(before == rank_of_row.astype(F32), hit, 0.0)
    return chosen, scale


def dispatch_kernel(slots, old_ref, new_ref, ids_ref, tok_ref, out_ref):
    rows = slots * CAP
    row = lax.broadcasted_iota(jnp.int32, (rows, 1), 0)
    chosen, _ = route_rows(
        ids_ref[...], None, old_ref, new_ref, rows, slots, row // CAP, row % CAP
    )
    picked = dot(chosen.astype(BF), tok_ref[...]).astype(BF)
    for slot in range(slots):
        out_ref[slot] = picked[slot * CAP : (slot + 1) * CAP, :]


def combine_kernel(
    slots, parts, old_ref, new_ref, ids_ref, weight_ref, back_ref, *rest
):
    sums, (out_ref, rows_ref) = rest[:-2], rest[-2:]
    rows = slots * parts * CAP
    row = lax.broadcasted_iota(jnp.int32, (rows, 1), 0)
    chosen, scale = route_rows(
        ids_ref[...],
        weight_ref[...],
        old_ref,
        new_ref,
        rows,
        slots,
        row // (parts * CAP),
        row % CAP,
    )
    mix = chosen * scale
    high = mix.astype(BF)
    low = (mix - high.astype(F32)).astype(BF)
    for block in range(slots * parts):
        rows_ref[block * CAP : (block + 1) * CAP, :] = back_ref[block]
    dims = (((0,), (0,)), ((), ()))
    total = lax.dot_general(high, rows_ref[...], dims, preferred_element_type=F32)
    total = total + lax.dot_general(low, rows_ref[...], dims, preferred_element_type=F32)
    for term in sums:
        total = total + term[...].astype(F32)
    out_ref[...] = total.astype(BF)


def shared_first_kernel(
    chips,
    steps,
    place_ref,
    tok_ref,
    gate_ref,
    up_ref,
    down_ref,
    send_ref,
    keep_ref,
    hidden_ref,
    gate_buf,
    up_buf,
    down_buf,
    gate_acc,
    up_acc,
    gate_sem,
    up_sem,
    down_sem,
):
    depth = gate_ref.shape[0] // steps
    width = send_ref.shape[2]
    gates, ups, downs = [], [], []
    for step in range(steps):
        part = pl.ds(step * depth, depth)
        gates.append(
            pltpu.make_async_copy(gate_ref.at[part], gate_buf.at[part], gate_sem.at[step])
        )
        ups.append(pltpu.make_async_copy(up_ref.at[part], up_buf.at[part], up_sem.at[step]))
    for block in range(2 * (chips - 1)):
        columns = pl.ds(pl.multiple_of(place_ref[block] * width, width), width)
        downs.append(
            pltpu.make_async_copy(
                down_ref.at[:, columns], down_buf.at[block], down_sem.at[block]
            )
        )
    for copy in [c for pair in zip(gates, ups) for c in pair] + downs:
        copy.start()
    for step in range(steps):
        part = pl.ds(step * depth, depth)
        gates[step].wait()
        ups[step].wait()
        rows = tok_ref[:, part]
        gate_value = dot(rows, gate_buf[part, :])
        up_value = dot(rows, up_buf[part, :])
        if step:
            gate_value = gate_value + gate_acc[...]
            up_value = up_value + up_acc[...]
        if step < steps - 1:
            gate_acc[...] = gate_value
            up_acc[...] = up_value
        else:
            hidden_ref[...] = silu_mul(gate_value, up_value)
    for block in range(2 * (chips - 1)):
        downs[block].wait()
        target = send_ref if block % 2 == 0 else keep_ref
        target[block // 2] = dot(hidden_ref[...], down_buf[block]).astype(BF)


def shared_rest_kernel(place_ref, hidden_ref, down_ref, send_ref, keep_ref, down_buf, down_sem):
    width = send_ref.shape[1]
    downs = []
    for block in range(2):
        columns = pl.ds(pl.multiple_of(place_ref[block] * width, width), width)
        downs.append(
            pltpu.make_async_copy(
                down_ref.at[:, columns], down_buf.at[block], down_sem.at[block]
            )
        )
        downs[-1].start()
    for block, target in enumerate((send_ref, keep_ref)):
        downs[block].wait()
        target[...] = dot(hidden_ref[...], down_buf[block]).astype(BF)


def routed_kernel(
    steps,
    parts,
    in_ref,
    gate_ref,
    up_ref,
    down_ref,
    out_ref,
    rows_ref,
    gate_buf,
    up_buf,
    down_buf,
    gate_sem,
    up_sem,
    down_sem,
):
    depth = gate_ref.shape[1] // steps
    senders = in_ref.shape[0]
    width = out_ref.shape[2]
    gates, ups, downs = [], [], []
    for step in range(steps):
        part = pl.ds(step * depth, depth)
        gates.append(
            pltpu.make_async_copy(gate_ref.at[0, part], gate_buf.at[part], gate_sem.at[step])
        )
        ups.append(pltpu.make_async_copy(up_ref.at[0, part], up_buf.at[part], up_sem.at[step]))
    for part in range(parts):
        columns = pl.ds(part * width, width)
        downs.append(
            pltpu.make_async_copy(
                down_ref.at[0, :, columns], down_buf.at[part], down_sem.at[part]
            )
        )
    for copy in [c for pair in zip(gates, ups) for c in pair] + downs:
        copy.start()
    for sender in range(senders):
        rows_ref[sender * CAP : (sender + 1) * CAP, :] = in_ref[sender]
    gate_value = up_value = 0.0
    for step in range(steps):
        part = pl.ds(step * depth, depth)
        gates[step].wait()
        ups[step].wait()
        rows = rows_ref[:, part]
        gate_value = gate_value + dot(rows, gate_buf[part, :])
        up_value = up_value + dot(rows, up_buf[part, :])
    hidden = silu_mul(gate_value, up_value)
    for part in range(parts):
        downs[part].wait()
        value = dot(hidden, down_buf[part]).astype(BF)
        for sender in range(senders):
            out_ref[sender * parts + part] = value[sender * CAP : (sender + 1) * CAP, :]


def spec(space):
    return pl.BlockSpec(memory_space=space)


def local(
    tokens,
    expert_ids,
    combine_weight,
    old_plan,
    new_plan,
    gate_weight,
    up_weight,
    down_weight,
    shared_gate,
    shared_up,
    shared_down,
):
    slots = lax.axis_size("expert")
    parts = lax.axis_size("dp")
    chips = parts // 2
    tok, model = tokens.shape
    hidden_width = shared_gate.shape[1]
    width = model // parts
    steps = 8
    me = lax.axis_index("dp")
    chip, core = me // 2, me % 2
    ids = expert_ids.T
    weight = combine_weight.T
    dma = pltpu.SemaphoreType.DMA

    outgoing = pl.pallas_call(
        functools.partial(dispatch_kernel, slots),
        out_shape=jax.ShapeDtypeStruct((slots, CAP, model), BF),
        in_specs=[spec(SMEM), spec(SMEM), spec(VMEM), spec(VMEM)],
        out_specs=spec(VMEM),
        name="dispatch",
    )(old_plan, new_plan, ids, tokens)
    arrived = lax.all_to_all(outgoing, "expert", split_axis=0, concat_axis=0, tiled=True)

    others = [(chip + k) % chips for k in range(1, chips)]
    place_first = jnp.stack([q * 2 + b for q in others for b in (1 - core, core)])
    place_rest = jnp.stack([chip * 2 + 1 - core, chip * 2 + core])
    send, keep, hidden = pl.pallas_call(
        functools.partial(shared_first_kernel, chips, steps),
        out_shape=(
            jax.ShapeDtypeStruct((chips - 1, tok, width), BF),
            jax.ShapeDtypeStruct((chips - 1, tok, width), BF),
            jax.ShapeDtypeStruct((tok, hidden_width), BF),
        ),
        in_specs=[spec(SMEM), spec(VMEM), spec(ANY), spec(ANY), spec(ANY)],
        out_specs=(spec(VMEM),) * 3,
        scratch_shapes=[
            VMEM((model, hidden_width), BF),
            VMEM((model, hidden_width), BF),
            VMEM((2 * (chips - 1), hidden_width, width), BF),
            VMEM((tok, hidden_width), F32),
            VMEM((tok, hidden_width), F32),
            dma((steps,)),
            dma((steps,)),
            dma((2 * (chips - 1),)),
        ],
        name="shared_first",
        cost_estimate=pl.CostEstimate(
            flops=4 * tok * model * hidden_width + 2 * tok * hidden_width * model // 2,
            bytes_accessed=5 * model * hidden_width,
            transcendentals=0,
        ),
    )(place_first, tokens, shared_gate, shared_up, shared_down)

    pairs = [(j, j ^ 1) for j in range(parts)]
    partner = lax.ppermute(send, "dp", pairs)
    chip_sum = (partner.astype(F32) + keep.astype(F32)).astype(BF)
    sums = []
    for k in range(1, chips):
        moves = [(j, (j // 2 + k) % chips * 2 + j % 2) for j in range(parts)]
        sums.append(lax.ppermute(chip_sum[k - 1], "dp", moves))

    send_rest, keep_rest = pl.pallas_call(
        shared_rest_kernel,
        out_shape=(jax.ShapeDtypeStruct((tok, width), BF),) * 2,
        in_specs=[spec(SMEM), spec(VMEM), spec(ANY)],
        out_specs=(spec(VMEM),) * 2,
        scratch_shapes=[VMEM((2, hidden_width, width), BF), dma((2,))],
        name="shared_rest",
        cost_estimate=pl.CostEstimate(
            flops=4 * tok * hidden_width * width,
            bytes_accessed=4 * hidden_width * width,
            transcendentals=0,
        ),
    )(place_rest, hidden, shared_down)
    sums += [keep_rest, lax.ppermute(send_rest, "dp", pairs)]

    routed = pl.pallas_call(
        functools.partial(routed_kernel, steps, parts),
        out_shape=jax.ShapeDtypeStruct((slots * parts, CAP, width), BF),
        in_specs=[spec(VMEM), spec(ANY), spec(ANY), spec(ANY)],
        out_specs=spec(VMEM),
        scratch_shapes=[
            VMEM((slots * CAP, model), BF),
            VMEM((model, hidden_width), BF),
            VMEM((model, hidden_width), BF),
            VMEM((parts, hidden_width, width), BF),
            dma((steps,)),
            dma((steps,)),
            dma((parts,)),
        ],
        name="routed",
        cost_estimate=pl.CostEstimate(
            flops=6 * tok * model * hidden_width,
            bytes_accessed=6 * model * hidden_width,
            transcendentals=0,
        ),
    )(arrived, gate_weight, up_weight, down_weight)
    back = lax.all_to_all(routed, ("expert", "dp"), split_axis=0, concat_axis=0, tiled=True)

    return pl.pallas_call(
        functools.partial(combine_kernel, slots, parts),
        out_shape=jax.ShapeDtypeStruct((tok, width), BF),
        in_specs=[spec(SMEM), spec(SMEM)] + [spec(VMEM)] * (3 + len(sums)),
        out_specs=spec(VMEM),
        scratch_shapes=[VMEM((slots * parts * CAP, width), BF)],
        name="combine",
    )(old_plan, new_plan, ids, weight, back, *sums)


def solution(mesh):
    in_specs = (
        P("expert", None),
        P("expert", None),
        P("expert", None),
        P(),
        P(),
        P("expert", None, "dp"),
        P("expert", None, "dp"),
        P("expert", "dp", None),
        P(None, "dp"),
        P(None, "dp"),
        P("dp", None),
    )
    out_specs = P("expert", "dp")
    return jax.shard_map(local, mesh=mesh, in_specs=in_specs, out_specs=out_specs, check_vma=False)
```

time: 110 us -> 50.5 us (0.46)
  waiting for transfers between devices: 28.4 us -> 1.18 us
  Pallas kernels: 0 us -> 24.5 us
  local copies, waits for them, and re-layouts: 23.7 us -> 1.63 us
  matrix products: 20 us -> 0 us
  between operations: 13.7 us -> 0.06 us
  blocking collectives: 0 us -> 12.1 us
  other arithmetic: 11.2 us -> 1.34 us
  starting transfers between devices: 12.9 us -> 9.23 us
    pallas_call x0 -> x5, Pallas kernels: none -> 24.5 us  [the longest x1 7.64 us: local(): pl.pallas_call(functools.partial(shared_first_kernel, chips, steps), out_...]
    dot_general x5 -> x0, matrix products: 20 us -> none  [the longest x2 13.1 us: expert_block(): jnp.dot(hidden, down_part, preferred_element_type=jnp.float32)]
    reduce_scatter x2 -> x0, waiting for transfers between devices: 16 us -> none  [the longest x1 11.7 us: local(): lax.psum_scatter(slot_rows.astype(jnp.bfloat16), 'dp', scatter_dimension=...]
    gather x8 -> x0, local copies, waits for them, and re-layouts: 15.4 us -> none  [combine_routes(): picked = rows[row_index[:, route]].astype(jnp.float32)]
    all_to_all x0 -> x1, blocking collectives: none -> 12.1 us  [local(): lax.all_to_all(routed, ('expert', 'dp'), split_axis=0, concat_axis=0, til...]
    all_to_all x1 -> x0, waiting for transfers between devices: 6.88 us -> none  [local(): lax.all_to_all(slot_sum.reshape(slot_count, capacity, slot_sum.shape[1])....]
    all_to_all x1 -> x0, starting transfers between devices: 5.52 us -> none  [local(): lax.all_to_all(slot_sum.reshape(slot_count, capacity, slot_sum.shape[1])....]
    convert_element_type x4 -> x0, other arithmetic: 5.49 us -> none  [the longest x1 4.69 us: local(): mixed_out = (shared_sum + routed).astype(jnp.bfloat16)]
  transfers between devices with their start and end apart: 4 -> 4, of which waited for: 4 -> 1; matrix products, arithmetic and copies ran while one was open for 25% -> 1% of each run, Pallas kernels for 0% -> 28%
where the time goes in v1:
time: 50.5 us; the launch traced here: 50.1 us
  Pallas kernels  24.5 us (49%)
  blocking collectives  12.1 us (24%)
  starting transfers between devices  9.23 us (18%)
  local copies, waits for them, and re-layouts  1.63 us (3%)
  other arithmetic  1.34 us (3%)
  waiting for transfers between devices  1.18 us (2%)
    all_to_all x1, blocking collectives, local(): lax.all_to_all(routed, ('expert', 'dp'), split_axis=0, concat_axis=0, til...  12.1 us
    pallas_call x1, Pallas kernels, local(): pl.pallas_call(functools.partial(shared_first_kernel, chips, steps), out_...  7.64 us
    pallas_call x1, Pallas kernels, local(): pl.pallas_call(functools.partial(routed_kernel, steps, parts), out_shape=...  7.29 us
    all_to_all x1, starting transfers between devices, local(): lax.all_to_all(outgoing, 'expert', split_axis=0, concat_axis=0, tiled=True)  6.88 us
    pallas_call x1, Pallas kernels, local(): pl.pallas_call(shared_rest_kernel, out_shape=(jax.ShapeDtypeStruct((tok,...  3.87 us
    pallas_call x1, Pallas kernels, local(): pl.pallas_call(functools.partial(combine_kernel, slots, parts), out_shape...  2.95 us
    pallas_call x1, Pallas kernels, local(): pl.pallas_call(functools.partial(dispatch_kernel, slots), out_shape=jax.S...  2.77 us
    unnamed x8, local copies, waits for them, and re-layouts  1.63 us
  transfers between devices with their start and end apart: 4, of which 1 were waited for; matrix products, arithmetic and copies ran while one was open for 1% of the time, Pallas kernels for 28%

profile of v1, /device:TPU:0, one launch (start us, length us, event | category | flops | bytes accessed | tf_op | source)
XLA Modules:
  0.0 50.1 jit_solution(10145838632670324999)
XLA Ops:
  0.0 0.6 %pad_add_fusion.place_ref = s32[2]{0:T(128)} fusion(s32[1]{0:T(128)} %bitcast.3, s32[1]{0:T(128)} %bitcast.2), kind=kLoop, calls=%fused_computation.2 | loop fusion | flops 2 | bytes 16 | tf_op jit(solution)/shard_map/stack | solution.py:256
  0.6 7.6 %shared_first.1 = (bf16[1,256,1024]{2,1,0:T(8,128)(2,1)}, bf16[1,256,1024]{2,1,0:T(8,128)(2,1)}, bf16[256,512]{1,0:T(8,128)(2,1)}) custom-call(s32[2]{0:T(128)} %pad_add_fusion.place_ref, bf16[256,4096]{1,0:T(8,128)(2,1)} %tok_ref.3, bf16[4096,512]{1,0:T(8,128)(2,1)} %gate_ref.3, bf16[4096,512]{1,0:T(8,128)(2,1)} %up_ref.3, bf16[512,4096]{1,0:T(8,128)(2,1)} %down_ref.5), custom_call_target="tpu_custom_call" | custom-call | flops 2684354560 | bytes 10485760 | tf_op jit(solution)/shard_map/shared_first/pallas_call | solution.py:258
  8.2 0.0 copy-start.1
  8.2 0.6 %collective-permute-start = (bf16[1,256,1024]{2,1,0:T(8,128)(2,1)}, bf16[1,256,1024]{2,1,0:T(8,128)(2,1)S(1)}, u32[]{:S(2)}, u32[]{:S(2)}) collective-permute-start(bf16[1,256,1024]{2,1,0:T(8,128)(2,1)} %get-tuple-element.10), channel_id=1, source_target_pairs={{0,8},{8,0},{16,24},{24,16},{1,9},{9,1},{17,25},{25,17},{2,10},{10... | collective-permute-start | bytes 1572872 | tf_op jit(solution)/shard_map/ppermute | solution.py:286
  8.8 2.8 %dispatch.1 = bf16[8,2,4096]{2,1,0:T(2,128)(2,1)} custom-call(s32[8]{0:T(128)} %old_ref.3, s32[8]{0:T(128)} %new_ref.3, s32[8,256]{1,0:T(8,128)} %bitcast.8, bf16[256,4096]{1,0:T(8,128)(2,1)} %tok_ref.3), custom_call_target="tpu_custom_call" | custom-call | tf_op jit(solution)/shard_map/dispatch/pallas_call | solution.py:246
  11.6 6.9 %all-to-all-start = ((bf16[8,2,4096]{2,1,0:T(2,128)(2,1)}), bf16[8,2,4096]{2,1,0:T(2,128)(2,1)S(1)}, u32[]{:S(2)}, u32[]{:S(2)}) async-start(bf16[8,2,4096]{2,1,0:T(2,128)(2,1)} %dispatch.1), calls=%async_computation | async-start | bytes 262144 | tf_op jit(solution)/shard_map/all_to_all | solution.py:253
  18.5 0.6 %pad_add_fusion.1.place_ref = s32[2]{0:T(128)} fusion(s32[1]{0:T(128)} %bitcast.6, s32[1]{0:T(128)} %bitcast.5), kind=kLoop, calls=%fused_computation.3 | loop fusion | flops 2 | bytes 16 | tf_op jit(solution)/shard_map/stack | solution.py:257
  19.0 3.9 %shared_rest.1 = (bf16[256,1024]{1,0:T(8,128)(2,1)}, bf16[256,1024]{1,0:T(8,128)(2,1)}) custom-call(s32[2]{0:T(128)} %pad_add_fusion.1.place_ref, bf16[256,512]{1,0:T(8,128)(2,1)} %get-tuple-element.12.hidden_ref, bf16[512,4096]{1,0:T(8,128)(2,1)} %down_ref.5), custom_call_target="tpu_custom_call" | custom-call | flops 536870912 | bytes 2097152 | tf_op jit(solution)/shard_map/shared_rest/pallas_call | solution.py:293
  22.9 0.2 collective-permute-start.2
  23.1 0.0 collective-permute-done
  23.1 0.0 copy-done.1
  23.1 0.2 fusion
  23.3 1.6 %collective-permute-start.1 = (bf16[256,1024]{1,0:T(8,128)(2,1)S(1)}, bf16[256,1024]{1,0:T(8,128)(2,1)S(1)}, u32[]{:S(2)}, u32[]{:S(2)}) collective-permute-start(bf16[256,1024]{1,0:T(8,128)(2,1)S(1)} %fusion), channel_id=1, source_target_pairs={{0,16},{8,24},{16,0},{24,8},{1,17},{9,25},{17,1},{25,9},{2,18},{10... | collective-permute-start | bytes 1572872 | tf_op jit(solution)/shard_map/ppermute | solution.py:291
  24.9 1.2 %all-to-all-done.in_ref = bf16[8,2,4096]{2,1,0:T(2,128)(2,1)S(1)} async-done(((bf16[8,2,4096]{2,1,0:T(2,128)(2,1)}), bf16[8,2,4096]{2,1,0:T(2,128)(2,1)S(1)}, u32[]{:S(2)}, u32[]{:S(2)}) %all-to-all-start) | async-done | bytes 131104 | tf_op jit(solution)/shard_map/all_to_all | solution.py:253
  26.1 0.0 copy-start
  26.1 0.7 %copy-done = bf16[8,2,4096]{2,1,0:T(2,128)(2,1)} copy-done((bf16[8,2,4096]{2,1,0:T(2,128)(2,1)}, bf16[8,2,4096]{2,1,0:T(2,128)(2,1)S(1)}, u32[]{:S(2)}) %copy-start) | copy-done | bytes 131096
  26.7 7.3 %routed.1 = bf16[32,2,1024]{2,1,0:T(2,128)(2,1)} custom-call(bf16[8,2,4096]{2,1,0:T(2,128)(2,1)} %copy-done, bf16[1,4096,512]{2,1,0:T(8,128)(2,1)} %gate_ref.2, bf16[1,4096,512]{2,1,0:T(8,128)(2,1)} %up_ref.2, bf16[1,512,4096]{2,1,0:T(8,128)(2,1)} %down_ref.3), custom_call_target="tpu_custom_call" | custom-call | flops 3221225472 | bytes 12582912 | tf_op jit(solution)/shard_map/routed/pallas_call | solution.py:308
  34.0 12.1 %all_to_all.10.back_ref = bf16[32,2,1024]{2,1,0:T(2,128)(2,1)} all-to-all(bf16[32,2,1024]{2,1,0:T(2,128)(2,1)} %routed.1), channel_id=1, replica_groups=mesh['dp'=4,'expert'=8] {'expert','dp'}, dimensions={0} | all-to-all | bytes 262144 | tf_op jit(solution)/shard_map/all_to_all | solution.py:329
  46.1 0.0 collective-permute-done.2.rest_2_
  46.1 0.0 copy-start.2
  46.1 0.0 collective-permute-done.1.rest_0_
  46.1 0.0 copy-start.3
  46.1 0.8 %copy-done.2 = bf16[256,1024]{1,0:T(8,128)(2,1)} copy-done((bf16[256,1024]{1,0:T(8,128)(2,1)}, bf16[256,1024]{1,0:T(8,128)(2,1)S(1)}, u32[]{:S(2)}) %copy-start.2) | copy-done | bytes 524312
  47.0 0.1 copy-done.3
  47.1 2.9 %combine.1 = bf16[256,1024]{1,0:T(8,128)(2,1)} custom-call(s32[8]{0:T(128)} %old_ref.3, s32[8]{0:T(128)} %new_ref.3, s32[8,256]{1,0:T(8,128)} %bitcast.9, f32[8,256]{1,0:T(8,128)} %bitcast.10, bf16[32,2,1024]{2,1,0:T(2,128)(2,1)} %all_to_all.10.back_ref, bf16[256,1024]{1,0:T(8,128)(2,1)} %copy-done.3, bf16[256,1024]{1,0:T(8,128)(2,1)} %get-tuple-element.13.rest_1_, ...), custom_call_target="tpu_custom_call" | custom-call | tf_op jit(solution)/shard_map/combine/pallas_call | solution.py:331
Async XLA Ops:
  8.2 14.9 %copy-start.1 = (bf16[1,256,1024]{2,1,0:T(8,128)(2,1)S(1)}, bf16[1,256,1024]{2,1,0:T(8,128)(2,1)}, u32[]{:S(2)}) copy-start(bf16[1,256,1024]{2,1,0:T(8,128)(2,1)} %get-tuple-element.11) | copy-start | bytes 1572868
  8.2 14.9 %collective-permute-start = (bf16[1,256,1024]{2,1,0:T(8,128)(2,1)}, bf16[1,256,1024]{2,1,0:T(8,128)(2,1)S(1)}, u32[]{:S(2)}, u32[]{:S(2)}) collective-permute-start(bf16[1,256,1024]{2,1,0:T(8,128)(2,1)} %get-tuple-element.10), channel_id=1, source_target_pairs={{0,8},{8,0},{16,24},{24,16},{1,9},{9,1},{17,25},{25,17},{2,10},{10... | collective-permute-start | bytes 1572872 | tf_op jit(solution)/shard_map/ppermute | solution.py:286
  11.6 14.5 %all-to-all-start = ((bf16[8,2,4096]{2,1,0:T(2,128)(2,1)}), bf16[8,2,4096]{2,1,0:T(2,128)(2,1)S(1)}, u32[]{:S(2)}, u32[]{:S(2)}) async-start(bf16[8,2,4096]{2,1,0:T(2,128)(2,1)} %dispatch.1), calls=%async_computation | async-start | bytes 262144 | tf_op jit(solution)/shard_map/all_to_all | solution.py:253
  22.9 23.2 %collective-permute-start.2 = (bf16[256,1024]{1,0:T(8,128)(2,1)}, bf16[256,1024]{1,0:T(8,128)(2,1)S(1)}, u32[]{:S(2)}, u32[]{:S(2)}) collective-permute-start(bf16[256,1024]{1,0:T(8,128)(2,1)} %get-tuple-element.14), channel_id=1, source_target_pairs={{0,8},{8,0},{16,24},{24,16},{1,9},{9,1},{17,25},{25,17},{2,10},{10... | collective-permute-start | bytes 1572872 | tf_op jit(solution)/shard_map/ppermute | solution.py:306
  23.3 22.8 %collective-permute-start.1 = (bf16[256,1024]{1,0:T(8,128)(2,1)S(1)}, bf16[256,1024]{1,0:T(8,128)(2,1)S(1)}, u32[]{:S(2)}, u32[]{:S(2)}) collective-permute-start(bf16[256,1024]{1,0:T(8,128)(2,1)S(1)} %fusion), channel_id=1, source_target_pairs={{0,16},{8,24},{16,0},{24,8},{1,17},{9,25},{17,1},{25,9},{2,18},{10... | collective-permute-start | bytes 1572872 | tf_op jit(solution)/shard_map/ppermute | solution.py:291
  26.1 0.7 %copy-start = (bf16[8,2,4096]{2,1,0:T(2,128)(2,1)}, bf16[8,2,4096]{2,1,0:T(2,128)(2,1)S(1)}, u32[]{:S(2)}) copy-start(bf16[8,2,4096]{2,1,0:T(2,128)(2,1)S(1)} %all-to-all-done.in_ref) | copy-start | bytes 393220
  46.1 0.8 %copy-start.2 = (bf16[256,1024]{1,0:T(8,128)(2,1)}, bf16[256,1024]{1,0:T(8,128)(2,1)S(1)}, u32[]{:S(2)}) copy-start(bf16[256,1024]{1,0:T(8,128)(2,1)S(1)} %collective-permute-done.2.rest_2_) | copy-start | bytes 1572868
  46.1 1.0 %copy-start.3 = (bf16[256,1024]{1,0:T(8,128)(2,1)}, bf16[256,1024]{1,0:T(8,128)(2,1)S(1)}, u32[]{:S(2)}) copy-start(bf16[256,1024]{1,0:T(8,128)(2,1)S(1)} %collective-permute-done.1.rest_0_) | copy-start | bytes 1572868

commit v2 on v0

v2 whole, which is shorter than its diff:
```python
import functools

import jax
import jax.numpy as jnp
from jax import lax
from jax.experimental import pallas as pl
from jax.experimental.pallas import tpu as pltpu
from jax.sharding import PartitionSpec as P


CAP = 2
BF = jnp.bfloat16
F32 = jnp.float32
VMEM = pltpu.VMEM
ANY = pl.ANY
SMEM = pltpu.SMEM


def silu_mul(gate_value, up_value):
    return (gate_value / (1.0 + jnp.exp(-gate_value)) * up_value).astype(BF)


def dot(a, b):
    return jnp.dot(a, b, preferred_element_type=F32)


def route_rows(ids, weight, old_ref, new_ref, slot_of, span, slots, ranks):
    tok = ids.shape[1]
    rows = slots * span * ranks
    row = lax.broadcasted_iota(jnp.int32, (rows, 1), 0)
    block, rank = row // (span * ranks), row % ranks
    plan = jnp.full((rows, 1), -1, jnp.int32)
    for index in range(slots):
        slot = slot_of(index)
        expert = old_ref[slot]
        present = (new_ref[slot] == expert) | (new_ref[lax.rem(slot + 1, slots)] == expert)
        plan = jnp.where(block == index, jnp.where(present, expert, -1), plan)
    hit = jnp.zeros((rows, tok), F32)
    scale = jnp.zeros((rows, tok), F32)
    for k in range(ids.shape[0]):
        same = ids[k : k + 1, :] == plan
        hit = jnp.where(same, 1.0, hit)
        if weight is not None:
            scale = jnp.where(same, weight[k : k + 1, :], scale)
    earlier = lax.broadcasted_iota(jnp.int32, (tok, tok), 0)
    later = lax.broadcasted_iota(jnp.int32, (tok, tok), 1)
    before = dot(hit.astype(BF), jnp.where(earlier < later, 1.0, 0.0).astype(BF))
    chosen = jnp.where(before == rank.astype(F32), hit, 0.0)
    return chosen, scale


def ready_kernel(out_ref):
    out_ref[...] = jnp.zeros_like(out_ref)


def select_kernel(slots, old_ref, new_ref, ids_ref, after_ref, chosen_ref):
    me = lax.axis_index("expert")
    chosen, _ = route_rows(
        ids_ref[...], None, old_ref, new_ref, lambda k: me ^ k, 1, slots, CAP
    )
    chosen_ref[...] = chosen.astype(BF)


def pick_kernel(slots, chosen_ref, tok_ref, own_ref, send_ref):
    picked = dot(chosen_ref[...], tok_ref[...]).astype(BF)
    half = slots // 2
    for k in range(slots):
        target = own_ref if k < half else send_ref
        target[k % half] = picked[k * CAP : (k + 1) * CAP, :]


def pack_kernel(places, *refs):
    for target, (array, index) in enumerate(places):
        refs[-1][target] = refs[array][index]


def add_kernel(a_ref, b_ref, out_ref):
    out_ref[...] = (a_ref[...].astype(F32) + b_ref[...].astype(F32)).astype(BF)


def mix_kernel(slots, parts, old_ref, new_ref, ids_ref, weight_ref, after_ref, high_ref, low_ref):
    chosen, scale = route_rows(
        ids_ref[...], weight_ref[...], old_ref, new_ref, lambda k: k, parts, slots, CAP
    )
    mix = chosen * scale
    high = mix.astype(BF)
    high_ref[...] = high
    low_ref[...] = (mix - high.astype(F32)).astype(BF)


def combine_kernel(blocks, high_ref, low_ref, back_ref, *rest):
    sums, (out_ref, rows_ref) = rest[:-2], rest[-2:]
    for block in range(blocks):
        rows_ref[block * CAP : (block + 1) * CAP, :] = back_ref[block]
    dims = (((0,), (0,)), ((), ()))
    total = lax.dot_general(high_ref[...], rows_ref[...], dims, preferred_element_type=F32)
    total = total + lax.dot_general(low_ref[...], rows_ref[...], dims, preferred_element_type=F32)
    for term in sums:
        total = total + term[...].astype(F32)
    out_ref[...] = total.astype(BF)


def column_block(chip, core, width):
    return pl.ds(pl.multiple_of((chip * 2 + core) * width, width), width)


def shared_first_kernel(
    chips, tok_ref, gate_ref, up_ref, down_ref, after_ref, send_ref, keep_ref, hidden_ref
):
    width = send_ref.shape[2]
    me = lax.axis_index("dp")
    chip, core = me // 2, me % 2
    hidden_ref[...] = silu_mul(dot(tok_ref[...], gate_ref[...]), dot(tok_ref[...], up_ref[...]))
    for k in range(1, chips):
        other = lax.rem(chip + k, chips)
        for target, side in ((send_ref, 1 - core), (keep_ref, core)):
            block = down_ref[:, column_block(other, side, width)]
            target[k - 1] = dot(hidden_ref[...], block).astype(BF)


def shared_rest_kernel(hidden_ref, down_ref, after_ref, send_ref, keep_ref):
    width = send_ref.shape[1]
    me = lax.axis_index("dp")
    chip, core = me // 2, me % 2
    for target, side in ((send_ref, 1 - core), (keep_ref, core)):
        block = down_ref[:, column_block(chip, side, width)]
        target[...] = dot(hidden_ref[...], block).astype(BF)


def routed_kernel(parts, places, *refs):
    arrays, (gate_ref, up_ref, down_ref, out_ref, rows_ref) = refs[:-5], refs[-5:]
    width = out_ref.shape[2]
    me = lax.axis_index("expert")
    for k, (array, index) in enumerate(places):
        rows_ref[k * CAP : (k + 1) * CAP, :] = arrays[array][index]
    rows = rows_ref[...]
    hidden = silu_mul(dot(rows, gate_ref[0]), dot(rows, up_ref[0]))
    for part in range(parts):
        value = dot(hidden, down_ref[0, :, part * width : (part + 1) * width]).astype(BF)
        for k in range(len(places)):
            out_ref[(me ^ k) * parts + part] = value[k * CAP : (k + 1) * CAP, :]


def cost(flops, size):
    return pl.CostEstimate(flops=flops, bytes_accessed=size, transcendentals=0)


def params(megabytes):
    return pltpu.CompilerParams(vmem_limit_bytes=megabytes * 1024 * 1024)


def spec(space):
    return pl.BlockSpec(memory_space=space)


def local(
    tokens,
    expert_ids,
    combine_weight,
    old_plan,
    new_plan,
    gate_weight,
    up_weight,
    down_weight,
    shared_gate,
    shared_up,
    shared_down,
):
    slots = lax.axis_size("expert")
    parts = lax.axis_size("dp")
    chips = parts // 2
    tok, model = tokens.shape
    hidden_width = shared_gate.shape[1]
    width = model // parts
    ids = expert_ids.T
    weight = combine_weight.T
    rows = jax.ShapeDtypeStruct((tok, width), BF)

    half = slots // 2
    blocks = jax.ShapeDtypeStruct((half, CAP, model), BF)
    ready = pl.pallas_call(
        ready_kernel,
        out_shape=jax.ShapeDtypeStruct((8, 128), F32),
        out_specs=spec(VMEM),
        name="ready",
        cost_estimate=cost(20 * tok * model * hidden_width, 0),
        compiler_params=params(1),
    )()
    chosen = pl.pallas_call(
        functools.partial(select_kernel, slots),
        out_shape=jax.ShapeDtypeStruct((slots * CAP, tok), BF),
        in_specs=[spec(SMEM), spec(SMEM), spec(VMEM), spec(ANY)],
        out_specs=spec(VMEM),
        name="select",
        cost_estimate=cost(2 * slots * CAP * tok * tok, 2 * tok * model),
        compiler_params=params(2),
    )(old_plan, new_plan, ids, ready)
    own, moving = pl.pallas_call(
        functools.partial(pick_kernel, slots),
        out_shape=(blocks, blocks),
        in_specs=[spec(VMEM), spec(VMEM)],
        out_specs=(spec(VMEM),) * 2,
        name="pick",
        cost_estimate=cost(2 * slots * CAP * tok * model, 2 * tok * model),
        compiler_params=params(4),
    )(chosen, tokens)
    arrays, places = [own], {k: (0, k) for k in range(half)}
    sent, bit = list(range(half, slots)), half
    while bit:
        turn = [(e, e ^ bit) for e in range(slots)]
        arrays.append(lax.ppermute(moving, "expert", turn))
        places.update({k: (len(arrays) - 1, index) for index, k in enumerate(sent)})
        bit //= 2
        if bit:
            sent = [k for k in range(slots) if k & bit]
            moving = pl.pallas_call(
                functools.partial(pack_kernel, [places[k] for k in sent]),
                out_shape=blocks,
                in_specs=[spec(VMEM)] * len(arrays),
                out_specs=spec(VMEM),
                name="pack",
                cost_estimate=cost(0, 4 * half * CAP * model),
                compiler_params=params(4),
            )(*arrays)
    places = [places[k] for k in range(slots)]

    send, keep, hidden = pl.pallas_call(
        functools.partial(shared_first_kernel, chips),
        out_shape=(
            jax.ShapeDtypeStruct((chips - 1, tok, width), BF),
            jax.ShapeDtypeStruct((chips - 1, tok, width), BF),
            jax.ShapeDtypeStruct((tok, hidden_width), BF),
        ),
        in_specs=[spec(VMEM)] * 4 + [spec(ANY)],
        out_specs=(spec(VMEM),) * 3,
        name="shared_first",
        cost_estimate=cost(4 * tok * model * hidden_width + 2 * tok * hidden_width * model // 2, 5 * model * hidden_width),
        compiler_params=params(20),
    )(tokens, shared_gate, shared_up, shared_down, own)

    pairs = [(j, j ^ 1) for j in range(parts)]
    partner = lax.ppermute(send, "dp", pairs)
    chip_sum = pl.pallas_call(
        add_kernel,
        out_shape=jax.ShapeDtypeStruct(keep.shape, BF),
        in_specs=[spec(VMEM)] * 2,
        out_specs=spec(VMEM),
        name="add",
        cost_estimate=cost(0, 6 * keep.size),
        compiler_params=params(4),
    )(partner, keep)
    sums = []
    for k in range(1, chips):
        moves = [(j, (j // 2 + k) % chips * 2 + j % 2) for j in range(parts)]
        sums.append(lax.ppermute(chip_sum[k - 1], "dp", moves))

    routed = pl.pallas_call(
        functools.partial(routed_kernel, parts, places),
        out_shape=jax.ShapeDtypeStruct((slots * parts, CAP, width), BF),
        in_specs=[spec(VMEM)] * (len(arrays) + 3),
        out_specs=spec(VMEM),
        scratch_shapes=[VMEM((slots * CAP, model), BF)],
        name="routed",
        cost_estimate=cost(2 * tok * model * hidden_width, 6 * model * hidden_width),
        compiler_params=params(20),
    )(*arrays, gate_weight, up_weight, down_weight)
    back = lax.all_to_all(
        routed, ("expert", "dp"), split_axis=0, concat_axis=0, tiled=True
    )

    send_rest, keep_rest = pl.pallas_call(
        shared_rest_kernel,
        out_shape=(rows, rows),
        in_specs=[spec(VMEM)] * 2 + [spec(ANY)],
        out_specs=(spec(VMEM),) * 2,
        name="shared_rest",
        cost_estimate=cost(4 * tok * hidden_width * width, 4 * hidden_width * width),
        compiler_params=params(12),
    )(hidden, shared_down, routed)
    sums += [keep_rest, lax.ppermute(send_rest, "dp", pairs)]

    mix = jax.ShapeDtypeStruct((slots * parts * CAP, tok), BF)
    high, low = pl.pallas_call(
        functools.partial(mix_kernel, slots, parts),
        out_shape=(mix, mix),
        in_specs=[spec(SMEM), spec(SMEM), spec(VMEM), spec(VMEM), spec(ANY)],
        out_specs=(spec(VMEM),) * 2,
        name="mix",
        compiler_params=params(8),
    )(old_plan, new_plan, ids, weight, routed)

    return pl.pallas_call(
        functools.partial(combine_kernel, slots * parts),
        out_shape=rows,
        in_specs=[spec(VMEM)] * (3 + len(sums)),
        out_specs=spec(VMEM),
        scratch_shapes=[VMEM((slots * parts * CAP, width), BF)],
        name="combine",
        compiler_params=params(12),
    )(high, low, back, *sums)


def solution(mesh):
    in_specs = (
        P("expert", None),
        P("expert", None),
        P("expert", None),
        P(),
        P(),
        P("expert", None, "dp"),
        P("expert", None, "dp"),
        P("expert", "dp", None),
        P(None, "dp"),
        P(None, "dp"),
        P("dp", None),
    )
    out_specs = P("expert", "dp")
    return jax.shard_map(local, mesh=mesh, in_specs=in_specs, out_specs=out_specs, check_vma=False)
```

time: 110 us -> 46.9 us (0.43)
  matrix products: 20 us -> 0 us
  local copies, waits for them, and re-layouts: 23.7 us -> 4.15 us
  between operations: 13.7 us -> 0.1 us
  other arithmetic: 11.2 us -> 0 us
  Pallas kernels: 0 us -> 9.46 us
  waiting for transfers between devices: 28.4 us -> 19.9 us
    dot_general x5 -> x0, matrix products: 20 us -> none  [the longest x2 13.1 us: expert_block(): jnp.dot(hidden, down_part, preferred_element_type=jnp.float32)]
    reduce_scatter x2 -> x0, waiting for transfers between devices: 16 us -> none  [the longest x1 11.7 us: local(): lax.psum_scatter(slot_rows.astype(jnp.bfloat16), 'dp', scatter_dimension=...]
    gather x8 -> x0, local copies, waits for them, and re-layouts: 15.4 us -> none  [combine_routes(): picked = rows[row_index[:, route]].astype(jnp.float32)]
    ppermute x0 -> x6, waiting for transfers between devices: none -> 10.3 us  [the longest x3 10.3 us: local(): arrays.append(lax.ppermute(moving, 'expert', turn))]
    pallas_call x0 -> x11, Pallas kernels: none -> 9.46 us  [the longest x1 2.95 us: local(): pl.pallas_call(functools.partial(shared_first_kernel, chips), out_shape=(...]
    ppermute x0 -> x6, starting transfers between devices: none -> 8.21 us  [the longest x3 5.97 us: local(): arrays.append(lax.ppermute(moving, 'expert', turn))]
    all_to_all x2 -> x1, starting transfers between devices: 12.8 us -> 4.81 us  [local(): lax.all_to_all(routed, ('expert', 'dp'), split_axis=0, concat_axis=0, til...]
    convert_element_type x4 -> x0, other arithmetic: 5.49 us -> none  [the longest x1 4.69 us: local(): mixed_out = (shared_sum + routed).astype(jnp.bfloat16)]
  transfers between devices with their start and end apart: 4 -> 7, of which waited for: 4 -> 4; matrix products, arithmetic and copies ran while one was open for 25% -> 0% of each run, Pallas kernels for 0% -> 9%
where the time goes in v2:
time: 46.9 us; the launch traced here: 46.7 us
  waiting for transfers between devices  19.9 us (42%)
  starting transfers between devices  13 us (28%)
  Pallas kernels  9.46 us (20%)
  local copies, waits for them, and re-layouts  4.15 us (9%)
    ppermute x3, waiting for transfers between devices, local(): arrays.append(lax.ppermute(moving, 'expert', turn))  10.3 us
    all_to_all x1, waiting for transfers between devices, local(): lax.all_to_all(routed, ('expert', 'dp'), split_axis=0, concat_axis=0, til...  9.63 us
    ppermute x3, starting transfers between devices, local(): arrays.append(lax.ppermute(moving, 'expert', turn))  5.97 us
    all_to_all x1, starting transfers between devices, local(): lax.all_to_all(routed, ('expert', 'dp'), split_axis=0, concat_axis=0, til...  4.81 us
    unnamed x22, local copies, waits for them, and re-layouts  4.15 us
    pallas_call x1, Pallas kernels, local(): pl.pallas_call(functools.partial(shared_first_kernel, chips), out_shape=(...  2.95 us
    pallas_call x1, Pallas kernels, local(): pl.pallas_call(functools.partial(routed_kernel, parts, places), out_shape...  2.49 us
    ppermute x1, starting transfers between devices, local(): sums.append(lax.ppermute(chip_sum[k - 1], 'dp', moves))  1.61 us
  transfers between devices with their start and end apart: 7, of which 4 were waited for; matrix products, arithmetic and copies ran while one was open for 0% of the time, Pallas kernels for 9%

profile of v2, /device:TPU:0, one launch (start us, length us, event | category | flops | bytes accessed | tf_op | source)
XLA Modules:
  0.0 46.7 jit_solution(2950212745624278511)
XLA Ops:
  0.0 0.0 copy-start.10
  0.0 0.0 copy-start.9
  0.0 0.0 copy-start.7
  0.0 0.0 copy-start.1
  0.0 0.0 copy-start
  0.0 0.0 copy-start.2
  0.0 0.0 copy-start.3
  0.0 0.6 %copy-done.10 = s32[8]{0:T(128)S(1)} copy-done((s32[8]{0:T(128)S(1)}, s32[8]{0:T(128)}, u32[]{:S(2)}) %copy-start.10) | copy-done | bytes 56
  0.7 0.0 copy-done.9
  0.7 0.1 copy-done.7
  0.7 0.7 %select.1.chosen_ref = bf16[16,256]{1,0:T(8,128)(2,1)S(1)} custom-call(s32[8]{0:T(128)S(1)} %copy-done.9, s32[8]{0:T(128)S(1)} %copy-done.10, s32[8,256]{1,0:T(8,128)S(1)} %bitcast.4, f32[8,128]{1,0:T(8,128)S(1)} %ready.1.after_ref), custom_call_target="tpu_custom_call" | custom-call | flops 2097152 | bytes 2097152 | tf_op jit(solution)/shard_map/select/pallas_call | solution.py:189
  1.4 0.2 copy-done.1
  1.6 0.4 pick.1
  2.0 0.8 %copy-done = bf16[512,4096]{1,0:T(8,128)(2,1)S(1)} copy-done((bf16[512,4096]{1,0:T(8,128)(2,1)S(1)}, bf16[512,4096]{1,0:T(8,128)(2,1)}, u32[]{:S(2)}) %copy-start) | copy-done | bytes 4194328
  2.9 1.2 %copy-done.2 = bf16[4096,512]{1,0:T(8,128)(2,1)S(1)} copy-done((bf16[4096,512]{1,0:T(8,128)(2,1)S(1)}, bf16[4096,512]{1,0:T(8,128)(2,1)}, u32[]{:S(2)}) %copy-start.2) | copy-done | bytes 4194328
  4.1 1.2 %copy-done.3 = bf16[4096,512]{1,0:T(8,128)(2,1)S(1)} copy-done((bf16[4096,512]{1,0:T(8,128)(2,1)S(1)}, bf16[4096,512]{1,0:T(8,128)(2,1)}, u32[]{:S(2)}) %copy-start.3) | copy-done | bytes 4194328
  5.3 0.0 copy-start.4
  5.3 0.0 copy-start.5
  5.3 0.0 copy-start.6
  5.3 2.9 %shared_first.1 = (bf16[1,256,1024]{2,1,0:T(8,128)(2,1)S(1)}, bf16[1,256,1024]{2,1,0:T(8,128)(2,1)S(1)}, bf16[256,512]{1,0:T(8,128)(2,1)S(1)}) custom-call(bf16[256,4096]{1,0:T(8,128)(2,1)S(1)} %copy-done.1, bf16[4096,512]{1,0:T(8,128)(2,1)S(1)} %copy-done.2, bf16[4096,512]{1,0:T(8,128)(2,1)S(1)} %copy-done.3, bf16[512,4096]{1,0:T(8,128)(2,1)S(1)} %copy-done, ...), custom_call_target="tpu_custom_call" | custom-call | flops 2684354560 | bytes 10485760 | tf_op jit(solution)/shard_map/shared_first/pallas_call | solution.py:227
  8.2 0.6 %collective-permute-start.3 = (bf16[1,256,1024]{2,1,0:T(8,128)(2,1)S(1)}, bf16[1,256,1024]{2,1,0:T(8,128)(2,1)S(1)}, u32[]{:S(2)}, u32[]{:S(2)}) collective-permute-start(bf16[1,256,1024]{2,1,0:T(8,128)(2,1)S(1)} %get-tuple-element.18), channel_id=1, source_target_pairs={{0,8},{8,0},{16,24},{24,16},{1,9},{9,1},{17,25},{25,17},{2,10},{10... | collective-permute-start | bytes 1572872 | tf_op jit(solution)/shard_map/ppermute | solution.py:242
  8.8 3.7 %collective-permute-start = (bf16[4,2,4096]{2,1,0:T(2,128)(2,1)S(1)}, bf16[4,2,4096]{2,1,0:T(2,128)(2,1)S(1)}, u32[]{:S(2)}, u32[]{:S(2)}) collective-permute-start(bf16[4,2,4096]{2,1,0:T(2,128)(2,1)S(1)} %get-tuple-element.15), channel_id=1, source_target_pairs={{0,4},{1,5},{2,6},{3,7},{4,0},{5,1},{6,2},{7,3},{8,12},{9,13},{10,... | collective-permute-start | bytes 196616 | tf_op jit(solution)/shard_map/ppermute | solution.py:211
  12.4 4.1 %collective-permute-done.refs_1_ = bf16[4,2,4096]{2,1,0:T(2,128)(2,1)S(1)} collective-permute-done((bf16[4,2,4096]{2,1,0:T(2,128)(2,1)S(1)}, bf16[4,2,4096]{2,1,0:T(2,128)(2,1)S(1)}, u32[]{:S(2)}, u32[]{:S(2)}) %collective-permute-start) | collective-permute-done | bytes 65568 | tf_op jit(solution)/shard_map/ppermute | solution.py:211
  16.5 0.7 %collective-permute-start.1 = (bf16[4,2,4096]{2,1,0:T(2,128)(2,1)S(1)}, bf16[4,2,4096]{2,1,0:T(2,128)(2,1)S(1)}, u32[]{:S(2)}, u32[]{:S(2)}) collective-permute-start(bf16[4,2,4096]{2,1,0:T(2,128)(2,1)S(1)} %pack.2), channel_id=1, source_target_pairs={{0,2},{1,3},{2,0},{3,1},{4,6},{5,7},{6,4},{7,5},{8,10},{9,11},{10,... | collective-permute-start | bytes 196616 | tf_op jit(solution)/shard_map/ppermute | solution.py:211
  17.3 3.5 %collective-permute-done.1.refs_2_ = bf16[4,2,4096]{2,1,0:T(2,128)(2,1)S(1)} collective-permute-done((bf16[4,2,4096]{2,1,0:T(2,128)(2,1)S(1)}, bf16[4,2,4096]{2,1,0:T(2,128)(2,1)S(1)}, u32[]{:S(2)}, u32[]{:S(2)}) %collective-permute-start.1) | collective-permute-done | bytes 65568 | tf_op jit(solution)/shard_map/ppermute | solution.py:211
  20.8 1.6 %collective-permute-start.2 = (bf16[4,2,4096]{2,1,0:T(2,128)(2,1)S(1)}, bf16[4,2,4096]{2,1,0:T(2,128)(2,1)S(1)}, u32[]{:S(2)}, u32[]{:S(2)}) collective-permute-start(bf16[4,2,4096]{2,1,0:T(2,128)(2,1)S(1)} %pack.3), channel_id=1, source_target_pairs={{0,1},{1,0},{2,3},{3,2},{4,5},{5,4},{6,7},{7,6},{8,9},{9,8},{10,11... | collective-permute-start | bytes 196616 | tf_op jit(solution)/shard_map/ppermute | solution.py:211
  22.4 2.7 %collective-permute-done.2.refs_3_ = bf16[4,2,4096]{2,1,0:T(2,128)(2,1)S(1)} collective-permute-done((bf16[4,2,4096]{2,1,0:T(2,128)(2,1)S(1)}, bf16[4,2,4096]{2,1,0:T(2,128)(2,1)S(1)}, u32[]{:S(2)}, u32[]{:S(2)}) %collective-permute-start.2) | collective-permute-done | bytes 65568 | tf_op jit(solution)/shard_map/ppermute | solution.py:211
  25.1 0.0 copy-done.4
  25.1 0.0 copy-done.5
  25.1 0.0 copy-done.6
  25.1 2.5 %routed.1.after_ref = bf16[32,2,1024]{2,1,0:T(2,128)(2,1)} custom-call(bf16[4,2,4096]{2,1,0:T(2,128)(2,1)S(1)} %get-tuple-element.14.refs_0_.after_ref, bf16[4,2,4096]{2,1,0:T(2,128)(2,1)S(1)} %collective-permute-done.refs_1_, bf16[4,2,4096]{2,1,0:T(2,128)(2,1)S(1)} %collective-permute-done.1.refs_2_, ...), custom_call_target="tpu_custom_call" | custom-call | flops 1073741824 | bytes 12582912 | tf_op jit(solution)/shard_map/routed/pallas_call | solution.py:257
  27.6 0.0 copy-start.8
  27.6 0.7 %shared_rest.1 = (bf16[256,1024]{1,0:T(8,128)(2,1)S(1)}, bf16[256,1024]{1,0:T(8,128)(2,1)S(1)}) custom-call(bf16[256,512]{1,0:T(8,128)(2,1)S(1)} %get-tuple-element.20.hidden_ref, bf16[512,4096]{1,0:T(8,128)(2,1)S(1)} %copy-done, bf16[32,2,1024]{2,1,0:T(2,128)(2,1)} %routed.1.after_ref), custom_call_target="tpu_custom_call" | custom-call | flops 536870912 | bytes 2097152 | tf_op jit(solution)/shard_map/shared_rest/pallas_call | solution.py:271
  28.3 0.1 collective-permute-start.5
  28.4 0.0 collective-permute-done.3.a_ref
  28.4 0.1 add.1
  28.5 1.6 %collective-permute-start.4 = (bf16[256,1024]{1,0:T(8,128)(2,1)S(1)}, bf16[256,1024]{1,0:T(8,128)(2,1)S(1)}, u32[]{:S(2)}, u32[]{:S(2)}) collective-permute-start(bf16[256,1024]{1,0:T(8,128)(2,1)S(1)} %bitcast.3), channel_id=1, source_target_pairs={{0,16},{8,24},{16,0},{24,8},{1,17},{9,25},{17,1},{25,9},{2,18},{10... | collective-permute-start | bytes 1572872 | tf_op jit(solution)/shard_map/ppermute | solution.py:255
  30.1 4.8 %all-to-all-start = ((bf16[32,2,1024]{2,1,0:T(2,128)(2,1)}), bf16[32,2,1024]{2,1,0:T(2,128)(2,1)S(1)}, u32[]{:S(2)}, u32[]{:S(2)}) async-start(bf16[32,2,1024]{2,1,0:T(2,128)(2,1)} %routed.1.after_ref), calls=%async_computation | async-start | bytes 262144 | tf_op jit(solution)/shard_map/all_to_all | solution.py:267
  34.9 0.0 copy-done.8
  35.0 0.7 %mix.1 = (bf16[64,256]{1,0:T(8,128)(2,1)S(1)}, bf16[64,256]{1,0:T(8,128)(2,1)S(1)}) custom-call(s32[8]{0:T(128)S(1)} %copy-done.9, s32[8]{0:T(128)S(1)} %copy-done.10, s32[8,256]{1,0:T(8,128)S(1)} %bitcast.5, f32[8,256]{1,0:T(8,128)S(1)} %bitcast.6, bf16[32,2,1024]{2,1,0:T(2,128)(2,1)} %routed.1.after_ref), custom_call_target="tpu_custom_call" | custom-call | tf_op jit(solution)/shard_map/mix/pallas_call | solution.py:283
  35.7 9.6 %all-to-all-done.back_ref = bf16[32,2,1024]{2,1,0:T(2,128)(2,1)S(1)} async-done(((bf16[32,2,1024]{2,1,0:T(2,128)(2,1)}), bf16[32,2,1024]{2,1,0:T(2,128)(2,1)S(1)}, u32[]{:S(2)}, u32[]{:S(2)}) %all-to-all-start) | async-done | bytes 131104 | tf_op jit(solution)/shard_map/all_to_all | solution.py:267
  45.3 0.0 collective-permute-done.5.rest_2_
  45.3 0.0 collective-permute-done.4.rest_0_
  45.3 1.4 %combine.1 = bf16[256,1024]{1,0:T(8,128)(2,1)} custom-call(bf16[64,256]{1,0:T(8,128)(2,1)S(1)} %get-tuple-element.16.high_ref, bf16[64,256]{1,0:T(8,128)(2,1)S(1)} %get-tuple-element.17.low_ref, bf16[32,2,1024]{2,1,0:T(2,128)(2,1)S(1)} %all-to-all-done.back_ref, bf16[256,1024]{1,0:T(8,128)(2,1)S(1)} %collective-permute-done.4.rest_0_, ...), custom_call_target="tpu_custom_call" | custom-call | tf_op jit(solution)/shard_map/combine/pallas_call | solution.py:292
  (3 shorter events, 0.0 us)
Async XLA Ops:
  0.0 0.7 %copy-start.10 = (s32[8]{0:T(128)S(1)}, s32[8]{0:T(128)}, u32[]{:S(2)}) copy-start(s32[8]{0:T(128)} %new_ref.3) | copy-start | bytes 100
  0.0 0.7 %copy-start.9 = (s32[8]{0:T(128)S(1)}, s32[8]{0:T(128)}, u32[]{:S(2)}) copy-start(s32[8]{0:T(128)} %old_ref.3) | copy-start | bytes 100
  0.0 0.7 %copy-start.7 = (s32[256,8]{0,1:T(8,128)S(1)}, s32[256,8]{0,1:T(8,128)}, u32[]{:S(2)}) copy-start(s32[256,8]{0,1:T(8,128)} %param.12) | copy-start | bytes 24580
  0.0 1.6 %copy-start.1 = (bf16[256,4096]{1,0:T(8,128)(2,1)S(1)}, bf16[256,4096]{1,0:T(8,128)(2,1)}, u32[]{:S(2)}) copy-start(bf16[256,4096]{1,0:T(8,128)(2,1)} %tok_ref.3) | copy-start | bytes 6291460
  0.0 2.9 %copy-start = (bf16[512,4096]{1,0:T(8,128)(2,1)S(1)}, bf16[512,4096]{1,0:T(8,128)(2,1)}, u32[]{:S(2)}) copy-start(bf16[512,4096]{1,0:T(8,128)(2,1)} %down_ref.3) | copy-start | bytes 12582916
  0.0 4.1 %copy-start.2 = (bf16[4096,512]{1,0:T(8,128)(2,1)S(1)}, bf16[4096,512]{1,0:T(8,128)(2,1)}, u32[]{:S(2)}) copy-start(bf16[4096,512]{1,0:T(8,128)(2,1)} %gate_ref.1) | copy-start | bytes 12582916
  0.0 5.2 %copy-start.3 = (bf16[4096,512]{1,0:T(8,128)(2,1)S(1)}, bf16[4096,512]{1,0:T(8,128)(2,1)}, u32[]{:S(2)}) copy-start(bf16[4096,512]{1,0:T(8,128)(2,1)} %up_ref.1) | copy-start | bytes 12582916
  5.3 19.8 %copy-start.4 = (bf16[1,4096,512]{2,1,0:T(8,128)(2,1)S(1)}, bf16[1,4096,512]{2,1,0:T(8,128)(2,1)}, u32[]{:S(2)}) copy-start(bf16[1,4096,512]{2,1,0:T(8,128)(2,1)} %refs_4_.1) | copy-start | bytes 12582916
  5.3 19.8 %copy-start.5 = (bf16[1,4096,512]{2,1,0:T(8,128)(2,1)S(1)}, bf16[1,4096,512]{2,1,0:T(8,128)(2,1)}, u32[]{:S(2)}) copy-start(bf16[1,4096,512]{2,1,0:T(8,128)(2,1)} %refs_5_.1) | copy-start | bytes 12582916
  5.3 19.8 %copy-start.6 = (bf16[1,512,4096]{2,1,0:T(8,128)(2,1)S(1)}, bf16[1,512,4096]{2,1,0:T(8,128)(2,1)}, u32[]{:S(2)}) copy-start(bf16[1,512,4096]{2,1,0:T(8,128)(2,1)} %refs_6_.1) | copy-start | bytes 12582916
  8.2 20.1 %collective-permute-start.3 = (bf16[1,256,1024]{2,1,0:T(8,128)(2,1)S(1)}, bf16[1,256,1024]{2,1,0:T(8,128)(2,1)S(1)}, u32[]{:S(2)}, u32[]{:S(2)}) collective-permute-start(bf16[1,256,1024]{2,1,0:T(8,128)(2,1)S(1)} %get-tuple-element.18), channel_id=1, source_target_pairs={{0,8},{8,0},{16,24},{24,16},{1,9},{9,1},{17,25},{25,17},{2,10},{10... | collective-permute-start | bytes 1572872 | tf_op jit(solution)/shard_map/ppermute | solution.py:242
  8.8 7.7 %collective-permute-start = (bf16[4,2,4096]{2,1,0:T(2,128)(2,1)S(1)}, bf16[4,2,4096]{2,1,0:T(2,128)(2,1)S(1)}, u32[]{:S(2)}, u32[]{:S(2)}) collective-permute-start(bf16[4,2,4096]{2,1,0:T(2,128)(2,1)S(1)} %get-tuple-element.15), channel_id=1, source_target_pairs={{0,4},{1,5},{2,6},{3,7},{4,0},{5,1},{6,2},{7,3},{8,12},{9,13},{10,... | collective-permute-start | bytes 196616 | tf_op jit(solution)/shard_map/ppermute | solution.py:211
  16.5 4.3 %collective-permute-start.1 = (bf16[4,2,4096]{2,1,0:T(2,128)(2,1)S(1)}, bf16[4,2,4096]{2,1,0:T(2,128)(2,1)S(1)}, u32[]{:S(2)}, u32[]{:S(2)}) collective-permute-start(bf16[4,2,4096]{2,1,0:T(2,128)(2,1)S(1)} %pack.2), channel_id=1, source_target_pairs={{0,2},{1,3},{2,0},{3,1},{4,6},{5,7},{6,4},{7,5},{8,10},{9,11},{10,... | collective-permute-start | bytes 196616 | tf_op jit(solution)/shard_map/ppermute | solution.py:211
  20.8 4.3 %collective-permute-start.2 = (bf16[4,2,4096]{2,1,0:T(2,128)(2,1)S(1)}, bf16[4,2,4096]{2,1,0:T(2,128)(2,1)S(1)}, u32[]{:S(2)}, u32[]{:S(2)}) collective-permute-start(bf16[4,2,4096]{2,1,0:T(2,128)(2,1)S(1)} %pack.3), channel_id=1, source_target_pairs={{0,1},{1,0},{2,3},{3,2},{4,5},{5,4},{6,7},{7,6},{8,9},{9,8},{10,11... | collective-permute-start | bytes 196616 | tf_op jit(solution)/shard_map/ppermute | solution.py:211
  27.6 7.4 %copy-start.8 = (f32[256,8]{0,1:T(8,128)S(1)}, f32[256,8]{0,1:T(8,128)}, u32[]{:S(2)}) copy-start(f32[256,8]{0,1:T(8,128)} %param.13) | copy-start | bytes 24580
  28.3 17.0 %collective-permute-start.5 = (bf16[256,1024]{1,0:T(8,128)(2,1)S(1)}, bf16[256,1024]{1,0:T(8,128)(2,1)S(1)}, u32[]{:S(2)}, u32[]{:S(2)}) collective-permute-start(bf16[256,1024]{1,0:T(8,128)(2,1)S(1)} %get-tuple-element.22), channel_id=1, source_target_pairs={{0,8},{8,0},{16,24},{24,16},{1,9},{9,1},{17,25},{25,17},{2,10},{10... | collective-permute-start | bytes 1572872 | tf_op jit(solution)/shard_map/ppermute | solution.py:280
  28.5 16.8 %collective-permute-start.4 = (bf16[256,1024]{1,0:T(8,128)(2,1)S(1)}, bf16[256,1024]{1,0:T(8,128)(2,1)S(1)}, u32[]{:S(2)}, u32[]{:S(2)}) collective-permute-start(bf16[256,1024]{1,0:T(8,128)(2,1)S(1)} %bitcast.3), channel_id=1, source_target_pairs={{0,16},{8,24},{16,0},{24,8},{1,17},{9,25},{17,1},{25,9},{2,18},{10... | collective-permute-start | bytes 1572872 | tf_op jit(solution)/shard_map/ppermute | solution.py:255
  30.1 15.2 %all-to-all-start = ((bf16[32,2,1024]{2,1,0:T(2,128)(2,1)}), bf16[32,2,1024]{2,1,0:T(2,128)(2,1)S(1)}, u32[]{:S(2)}, u32[]{:S(2)}) async-start(bf16[32,2,1024]{2,1,0:T(2,128)(2,1)} %routed.1.after_ref), calls=%async_computation | async-start | bytes 262144 | tf_op jit(solution)/shard_map/all_to_all | solution.py:267

commit v3 on v2

--- a/solution.py
+++ b/solution.py
@@ -24,13 +24,13 @@
     return jnp.dot(a, b, preferred_element_type=F32)
 
 
-def route_rows(ids, weight, old_ref, new_ref, slot_of, span, slots, ranks):
+def route_rows(ids, weight, old_ref, new_ref, slot_of, span, count, ranks, slots):
     tok = ids.shape[1]
-    rows = slots * span * ranks
+    rows = count * span * ranks
     row = lax.broadcasted_iota(jnp.int32, (rows, 1), 0)
     block, rank = row // (span * ranks), row % ranks
     plan = jnp.full((rows, 1), -1, jnp.int32)
-    for index in range(slots):
+    for index in range(count):
         slot = slot_of(index)
         expert = old_ref[slot]
         present = (new_ref[slot] == expert) | (new_ref[lax.rem(slot + 1, slots)] == expert)
@@ -53,20 +53,33 @@
     out_ref[...] = jnp.zeros_like(out_ref)
 
 
+def carried(index, quarter):
+    core = lax.axis_index("dp") % 2
+    offsets = (0, quarter, 2 * quarter + quarter * core)
+    return lax.axis_index("expert") ^ (index % quarter + offsets[index // quarter])
+
+
 def select_kernel(slots, old_ref, new_ref, ids_ref, after_ref, chosen_ref):
-    me = lax.axis_index("expert")
+    quarter = slots // 4
     chosen, _ = route_rows(
-        ids_ref[...], None, old_ref, new_ref, lambda k: me ^ k, 1, slots, CAP
+        ids_ref[...],
+        None,
+        old_ref,
+        new_ref,
+        lambda index: carried(index, quarter),
+        1,
+        3 * quarter,
+        CAP,
+        slots,
     )
     chosen_ref[...] = chosen.astype(BF)
 
 
-def pick_kernel(slots, chosen_ref, tok_ref, own_ref, send_ref):
+def pick_kernel(stays, moves, chosen_ref, tok_ref, own_ref, send_ref):
     picked = dot(chosen_ref[...], tok_ref[...]).astype(BF)
-    half = slots // 2
-    for k in range(slots):
-        target = own_ref if k < half else send_ref
-        target[k % half] = picked[k * CAP : (k + 1) * CAP, :]
+    for target, wanted in ((own_ref, stays), (send_ref, moves)):
+        for index, v in enumerate(wanted):
+            target[index] = picked[v * CAP : (v + 1) * CAP, :]
 
 
 def pack_kernel(places, *refs):
@@ -78,39 +91,58 @@
     out_ref[...] = (a_ref[...].astype(F32) + b_ref[...].astype(F32)).astype(BF)
 
 
-def mix_kernel(slots, parts, old_ref, new_ref, ids_ref, weight_ref, after_ref, high_ref, low_ref):
+def mix_kernel(slots, parts, old_ref, new_ref, ids_ref, weight_ref, after_ref, mix_ref):
     chosen, scale = route_rows(
-        ids_ref[...], weight_ref[...], old_ref, new_ref, lambda k: k, parts, slots, CAP
+        ids_ref[...], weight_ref[...], old_ref, new_ref, lambda k: k, parts, slots, CAP, slots
     )
     mix = chosen * scale
-    high = mix.astype(BF)
-    high_ref[...] = high
-    low_ref[...] = (mix - high.astype(F32)).astype(BF)
-
-
-def combine_kernel(blocks, high_ref, low_ref, back_ref, *rest):
-    sums, (out_ref, rows_ref) = rest[:-2], rest[-2:]
+    high = mix.astype(BF).astype(F32)
+    mix_ref[...] = jnp.concatenate([high, mix - high], axis=0).T.astype(BF)
+
+
+def total_kernel(a_ref, b_ref, *refs):
+    total = a_ref[...].astype(F32) + b_ref[...].astype(F32)
+    for term in refs[:-1]:
+        total = total + term[...].astype(F32)
+    refs[-1][...] = total
+
+
+def combine_kernel(blocks, pieces, mix_ref, back_ref, sum_ref, out_hbm, rows_ref, out_ref, sems):
     for block in range(blocks):
-        rows_ref[block * CAP : (block + 1) * CAP, :] = back_ref[block]
-    dims = (((0,), (0,)), ((), ()))
-    total = lax.dot_general(high_ref[...], rows_ref[...], dims, preferred_element_type=F32)
-    total = total + lax.dot_general(low_ref[...], rows_ref[...], dims, preferred_element_type=F32)
-    for term in sums:
-        total = total + term[...].astype(F32)
-    out_ref[...] = total.astype(BF)
+        pair = back_ref[block]
+        rows_ref[block * CAP : (block + 1) * CAP, :] = pair
+        rows_ref[(blocks + block) * CAP : (blocks + block + 1) * CAP, :] = pair
+    tall = out_ref.shape[0] // pieces
+    copies = []
+    for piece in range(pieces):
+        part = slice(piece * tall, (piece + 1) * tall)
+        total = dot(mix_ref[part, :], rows_ref[...]) + sum_ref[part, :]
+        out_ref[part, :] = total.astype(BF)
+        where = pl.ds(piece * tall, tall)
+        copies.append(
+            pltpu.make_async_copy(out_ref.at[where], out_hbm.at[where], sems.at[piece])
+        )
+        copies[-1].start()
+    for copy in copies:
+        copy.wait()
 
 
 def column_block(chip, core, width):
     return pl.ds(pl.multiple_of((chip * 2 + core) * width, width), width)
 
 
-def shared_first_kernel(
-    chips, tok_ref, gate_ref, up_ref, down_ref, after_ref, send_ref, keep_ref, hidden_ref
-):
+def shared_gate_kernel(tok_ref, gate_ref, after_ref, value_ref):
+    value_ref[...] = dot(tok_ref[...], gate_ref[...])
+
+
+def shared_up_kernel(tok_ref, up_ref, value_ref, hidden_ref):
+    hidden_ref[...] = silu_mul(value_ref[...], dot(tok_ref[...], up_ref[...]))
+
+
+def shared_first_kernel(chips, hidden_ref, down_ref, send_ref, keep_ref):
     width = send_ref.shape[2]
     me = lax.axis_index("dp")
     chip, core = me // 2, me % 2
-    hidden_ref[...] = silu_mul(dot(tok_ref[...], gate_ref[...]), dot(tok_ref[...], up_ref[...]))
     for k in range(1, chips):
         other = lax.rem(chip + k, chips)
         for target, side in ((send_ref, 1 - core), (keep_ref, core)):
@@ -130,15 +162,19 @@
 def routed_kernel(parts, places, *refs):
     arrays, (gate_ref, up_ref, down_ref, out_ref, rows_ref) = refs[:-5], refs[-5:]
     width = out_ref.shape[2]
+    quarter = len(places) // 4
     me = lax.axis_index("expert")
-    for k, (array, index) in enumerate(places):
-        rows_ref[k * CAP : (k + 1) * CAP, :] = arrays[array][index]
+    core = lax.axis_index("dp") % 2
+    offsets = (0, quarter, 2 * quarter + quarter * core, 3 * quarter - quarter * core)
+    for place, (array, index) in enumerate(places):
+        rows_ref[place * CAP : (place + 1) * CAP, :] = arrays[array][index]
     rows = rows_ref[...]
     hidden = silu_mul(dot(rows, gate_ref[0]), dot(rows, up_ref[0]))
     for part in range(parts):
         value = dot(hidden, down_ref[0, :, part * width : (part + 1) * width]).astype(BF)
-        for k in range(len(places)):
-            out_ref[(me ^ k) * parts + part] = value[k * CAP : (k + 1) * CAP, :]
+        for place in range(len(places)):
+            sender = me ^ (place % quarter + offsets[place // quarter])
+            out_ref[sender * parts + part] = value[place * CAP : (place + 1) * CAP, :]
 
 
 def cost(flops, size):
@@ -176,8 +212,16 @@
     weight = combine_weight.T
     rows = jax.ShapeDtypeStruct((tok, width), BF)
 
-    half = slots // 2
-    blocks = jax.ShapeDtypeStruct((half, CAP, model), BF)
+    quarter = slots // 4
+    virtual = range(3 * quarter)
+    pairs = [(j, j ^ 1) for j in range(parts)]
+    bits = [1 << n for n in range(quarter.bit_length() - 1)]
+    stays = [v for v in virtual if not v % quarter & bits[0]]
+    moves = [v for v in virtual if v % quarter & bits[0]]
+
+    def rows_of(count):
+        return jax.ShapeDtypeStruct((count, CAP, model), BF)
+
     ready = pl.pallas_call(
         ready_kernel,
         out_shape=jax.ShapeDtypeStruct((8, 128), F32),
@@ -188,7 +232,7 @@
     )()
     chosen = pl.pallas_call(
         functools.partial(select_kernel, slots),
-        out_shape=jax.ShapeDtypeStruct((slots * CAP, tok), BF),
+        out_shape=jax.ShapeDtypeStruct((3 * quarter * CAP, tok), BF),
         in_specs=[spec(SMEM), spec(SMEM), spec(VMEM), spec(ANY)],
         out_specs=spec(VMEM),
         name="select",
@@ -196,49 +240,75 @@
         compiler_params=params(2),
     )(old_plan, new_plan, ids, ready)
     own, moving = pl.pallas_call(
-        functools.partial(pick_kernel, slots),
-        out_shape=(blocks, blocks),
+        functools.partial(pick_kernel, stays, moves),
+        out_shape=(rows_of(len(stays)), rows_of(len(moves))),
         in_specs=[spec(VMEM), spec(VMEM)],
         out_specs=(spec(VMEM),) * 2,
         name="pick",
         cost_estimate=cost(2 * slots * CAP * tok * model, 2 * tok * model),
         compiler_params=params(4),
     )(chosen, tokens)
-    arrays, places = [own], {k: (0, k) for k in range(half)}
-    sent, bit = list(range(half, slots)), half
-    while bit:
-        turn = [(e, e ^ bit) for e in range(slots)]
-        arrays.append(lax.ppermute(moving, "expert", turn))
-        places.update({k: (len(arrays) - 1, index) for index, k in enumerate(sent)})
-        bit //= 2
-        if bit:
-            sent = [k for k in range(slots) if k & bit]
-            moving = pl.pallas_call(
-                functools.partial(pack_kernel, [places[k] for k in sent]),
-                out_shape=blocks,
-                in_specs=[spec(VMEM)] * len(arrays),
-                out_specs=spec(VMEM),
-                name="pack",
-                cost_estimate=cost(0, 4 * half * CAP * model),
-                compiler_params=params(4),
-            )(*arrays)
-    places = [places[k] for k in range(slots)]
-
-    send, keep, hidden = pl.pallas_call(
+    arrays, places = [own], {v: (0, index) for index, v in enumerate(stays)}
+
+    def pack(wanted):
+        return pl.pallas_call(
+            functools.partial(pack_kernel, [places[v] for v in wanted]),
+            out_shape=rows_of(len(wanted)),
+            in_specs=[spec(VMEM)] * len(arrays),
+            out_specs=spec(VMEM),
+            name="pack",
+            cost_estimate=cost(0, 4 * len(wanted) * CAP * model),
+            compiler_params=params(4),
+        )(*arrays)
+
+    for hop, bit in enumerate(bits, 1):
+        moves = [v for v in virtual if v % quarter & bit]
+        if hop > 1:
+            moving = pack(moves)
+        arrays.append(lax.ppermute(moving, "expert", [(e, e ^ bit) for e in range(slots)]))
+        places.update({v: (hop, index) for index, v in enumerate(moves)})
+    far = pack(virtual[2 * quarter :])
+    near = pack(virtual[quarter : 2 * quarter])
+    both = [(j, e) for j in range(parts) for e in range(slots)]
+    across = [(j * slots + e, j * slots + (e ^ (2 + j % 2) * quarter)) for j, e in both]
+    far = lax.ppermute(far, ("dp", "expert"), across)
+    near = lax.ppermute(near, "expert", [(e, e ^ quarter) for e in range(slots)])
+    swapped = lax.ppermute(far, "dp", pairs)
+    last = len(arrays)
+    arrays += [near, far, swapped]
+    places = [places[v] for v in range(quarter)]
+    places += [(last + group, index) for group in range(3) for index in range(quarter)]
+
+    gate_value = pl.pallas_call(
+        shared_gate_kernel,
+        out_shape=jax.ShapeDtypeStruct((tok, hidden_width), F32),
+        in_specs=[spec(VMEM)] * 2 + [spec(ANY)],
+        out_specs=spec(VMEM),
+        name="shared_gate",
+        cost_estimate=cost(2 * tok * model * hidden_width, 2 * model * hidden_width),
+        compiler_params=params(8),
+    )(tokens, shared_gate, own)
+    hidden = pl.pallas_call(
+        shared_up_kernel,
+        out_shape=jax.ShapeDtypeStruct((tok, hidden_width), BF),
+        in_specs=[spec(VMEM)] * 3,
+        out_specs=spec(VMEM),
+        name="shared_up",
+        cost_estimate=cost(2 * tok * model * hidden_width, 2 * model * hidden_width),
+        compiler_params=params(8),
+    )(tokens, shared_up, gate_value)
+    send, keep = pl.pallas_call(
         functools.partial(shared_first_kernel, chips),
-        out_shape=(
-            jax.ShapeDtypeStruct((chips - 1, tok, width), BF),
-            jax.ShapeDtypeStruct((chips - 1, tok, width), BF),
-            jax.ShapeDtypeStruct((tok, hidden_width), BF),
+        out_shape=(jax.ShapeDtypeStruct((chips - 1, tok, width), BF),) * 2,
+        in_specs=[spec(VMEM)] * 2,
+        out_specs=(spec(VMEM),) * 2,
+        name="shared_first",
+        cost_estimate=cost(
+            4 * (chips - 1) * tok * hidden_width * width, 4 * (chips - 1) * hidden_width * width
         ),
-        in_specs=[spec(VMEM)] * 4 + [spec(ANY)],
-        out_specs=(spec(VMEM),) * 3,
-        name="shared_first",
-        cost_estimate=cost(4 * tok * model * hidden_width + 2 * tok * hidden_width * model // 2, 5 * model * hidden_width),
-        compiler_params=params(20),
-    )(tokens, shared_gate, shared_up, shared_down, own)
-
-    pairs = [(j, j ^ 1) for j in range(parts)]
+        compiler_params=params(12),
+    )(hidden, shared_down)
+
     partner = lax.ppermute(send, "dp", pairs)
     chip_sum = pl.pallas_call(
         add_kernel,
@@ -279,25 +349,37 @@
     )(hidden, shared_down, routed)
     sums += [keep_rest, lax.ppermute(send_rest, "dp", pairs)]
 
-    mix = jax.ShapeDtypeStruct((slots * parts * CAP, tok), BF)
-    high, low = pl.pallas_call(
+    blocks = slots * parts
+    mix = pl.pallas_call(
         functools.partial(mix_kernel, slots, parts),
-        out_shape=(mix, mix),
+        out_shape=jax.ShapeDtypeStruct((tok, 2 * blocks * CAP), BF),
         in_specs=[spec(SMEM), spec(SMEM), spec(VMEM), spec(VMEM), spec(ANY)],
-        out_specs=(spec(VMEM),) * 2,
+        out_specs=spec(VMEM),
         name="mix",
         compiler_params=params(8),
     )(old_plan, new_plan, ids, weight, routed)
-
+    total = pl.pallas_call(
+        total_kernel,
+        out_shape=jax.ShapeDtypeStruct((tok, width), F32),
+        in_specs=[spec(VMEM)] * len(sums),
+        out_specs=spec(VMEM),
+        name="total",
+        compiler_params=params(8),
+    )(*sums)
+    pieces = 4
     return pl.pallas_call(
-        functools.partial(combine_kernel, slots * parts),
+        functools.partial(combine_kernel, blocks, pieces),
         out_shape=rows,
-        in_specs=[spec(VMEM)] * (3 + len(sums)),
-        out_specs=spec(VMEM),
-        scratch_shapes=[VMEM((slots * parts * CAP, width), BF)],
+        in_specs=[spec(VMEM)] * 3,
+        out_specs=spec(ANY),
+        scratch_shapes=[
+            VMEM((2 * blocks * CAP, width), BF),
+            VMEM((tok, width), BF),
+            pltpu.SemaphoreType.DMA((pieces,)),
+        ],
         name="combine",
         compiler_params=params(12),
-    )(high, low, back, *sums)
+    )(mix, back, total)
 
 
 def solution(mesh):

time: 46.9 us -> 41.5 us (0.88)
  waiting for transfers between devices: 19.9 us -> 14 us
  starting transfers between devices: 13 us -> 14 us
  local copies, waits for them, and re-layouts: 4.15 us -> 3.4 us
    all_to_all x1, waiting for transfers between devices: 9.63 us -> 0.95 us  [local(): lax.all_to_all(routed, ('expert', 'dp'), split_axis=0, concat_axis=0, til...]
    ppermute x1, waiting for transfers between devices: 0.01 us -> 8.38 us  [local(): sums.append(lax.ppermute(chip_sum[k - 1], 'dp', moves))]
    ppermute x3 -> x4, waiting for transfers between devices: 10.3 us -> 4.67 us  [the longest x1 2.33 us: local(): lax.ppermute(moving, 'expert', [(e, e ^ bit) for e in range(slots)])]
    pallas_call x5 -> x8, Pallas kernels: 2.47 us -> 4.97 us  [the longest x1 1.25 us: local(): pl.pallas_call(shared_up_kernel, out_shape=jax.ShapeDtypeStruct((tok, hid...]
    pallas_call x1, Pallas kernels: 2.95 us -> 0.71 us  [local(): pl.pallas_call(functools.partial(shared_first_kernel, chips), out_shape=(...]
    ppermute x3 -> x4, starting transfers between devices: 5.97 us -> 6.98 us  [the longest x1 2.82 us: local(): far = lax.ppermute(far, ('dp', 'expert'), across)]
    unnamed x22, local copies, waits for them, and re-layouts: 4.15 us -> 3.4 us
  transfers between devices with their start and end apart: 7 -> 8, of which waited for: 4 -> 5; matrix products, arithmetic and copies ran while one was open for 0% -> 0% of each run, Pallas kernels for 9% -> 10%
where the time goes in v3:
time: 41.5 us; the launch traced here: 41.3 us
  starting transfers between devices  14 us (34%)
  waiting for transfers between devices  14 us (34%)
  Pallas kernels  9.72 us (23%)
  local copies, waits for them, and re-layouts  3.4 us (8%)
    ppermute x1, waiting for transfers between devices, local(): sums.append(lax.ppermute(chip_sum[k - 1], 'dp', moves))  8.38 us
    all_to_all x1, starting transfers between devices, local(): lax.all_to_all(routed, ('expert', 'dp'), split_axis=0, concat_axis=0, til...  4.82 us
    unnamed x22, local copies, waits for them, and re-layouts  3.4 us
    ppermute x1, starting transfers between devices, local(): far = lax.ppermute(far, ('dp', 'expert'), across)  2.82 us
    ppermute x1, starting transfers between devices, local(): lax.ppermute(moving, 'expert', [(e, e ^ bit) for e in range(slots)])  2.58 us
    pallas_call x1, Pallas kernels, local(): pl.pallas_call(functools.partial(routed_kernel, parts, places), out_shape...  2.49 us
    ppermute x1, waiting for transfers between devices, local(): lax.ppermute(moving, 'expert', [(e, e ^ bit) for e in range(slots)])  2.33 us
    ppermute x1, waiting for transfers between devices, local(): lax.ppermute(near, 'expert', [(e, e ^ quarter) for e in range(slots)])  1.79 us
  transfers between devices with their start and end apart: 8, of which 5 were waited for; matrix products, arithmetic and copies ran while one was open for 0% of the time, Pallas kernels for 10%

profile of v3, /device:TPU:0, one launch (start us, length us, event | category | flops | bytes accessed | tf_op | source)
XLA Modules:
  0.0 41.3 jit_solution(1350163895195773739)
XLA Ops:
  0.0 0.0 copy-start.7
  0.0 0.0 copy-start.9
  0.0 0.0 copy-start.10
  0.0 0.0 copy-start
  0.0 0.0 copy-start.6
  0.0 0.0 copy-start.5
  0.0 0.7 %copy-done.7 = s32[256,8]{0,1:T(8,128)S(1)} copy-done((s32[256,8]{0,1:T(8,128)S(1)}, s32[256,8]{0,1:T(8,128)}, u32[]{:S(2)}) %copy-start.7) | copy-done | bytes 8216
  0.7 0.0 copy-done.9
  0.7 0.0 copy-done.10
  0.7 0.7 %select.1.chosen_ref = bf16[12,256]{1,0:T(8,128)(2,1)S(1)} custom-call(s32[8]{0:T(128)S(1)} %copy-done.9, s32[8]{0:T(128)S(1)} %copy-done.10, s32[8,256]{1,0:T(8,128)S(1)} %bitcast.4, f32[8,128]{1,0:T(8,128)S(1)} %ready.1.after_ref), custom_call_target="tpu_custom_call" | custom-call | flops 2097152 | bytes 2097152 | tf_op jit(solution)/shard_map/select/pallas_call | solution.py:233
  1.4 0.2 copy-done
  1.6 0.4 pick.1
  2.0 0.8 %copy-done.6 = bf16[4096,512]{1,0:T(8,128)(2,1)S(1)} copy-done((bf16[4096,512]{1,0:T(8,128)(2,1)S(1)}, bf16[4096,512]{1,0:T(8,128)(2,1)}, u32[]{:S(2)}) %copy-start.6) | copy-done | bytes 4194328
  2.9 0.0 copy-start.3
  2.9 0.0 copy-start.4
  2.9 1.2 %shared_gate.1.value_ref = f32[256,512]{1,0:T(8,128)S(1)} custom-call(bf16[256,4096]{1,0:T(8,128)(2,1)S(1)} %copy-done, bf16[4096,512]{1,0:T(8,128)(2,1)S(1)} %copy-done.6, bf16[3,2,4096]{2,1,0:T(2,128)(2,1)S(1)} %get-tuple-element.11.refs_0_.after_ref), custom_call_target="tpu_custom_call" | custom-call | flops 1073741824 | bytes 4194304 | tf_op jit(solution)/shard_map/shared_gate/pallas_call | solution.py:282
  4.1 0.0 copy-done.5
  4.1 0.0 copy-start.1
  4.1 0.0 copy-start.2
  4.1 1.3 %shared_up.1.hidden_ref = bf16[256,512]{1,0:T(8,128)(2,1)S(1)} custom-call(bf16[256,4096]{1,0:T(8,128)(2,1)S(1)} %copy-done, bf16[4096,512]{1,0:T(8,128)(2,1)S(1)} %copy-done.5, f32[256,512]{1,0:T(8,128)S(1)} %shared_gate.1.value_ref), custom_call_target="tpu_custom_call" | custom-call | flops 1073741824 | bytes 4194304 | tf_op jit(solution)/shard_map/shared_up/pallas_call | solution.py:291
  5.4 1.6 %copy-done.1 = bf16[512,4096]{1,0:T(8,128)(2,1)S(1)} copy-done((bf16[512,4096]{1,0:T(8,128)(2,1)S(1)}, bf16[512,4096]{1,0:T(8,128)(2,1)}, u32[]{:S(2)}) %copy-start.1) | copy-done | bytes 4194328
  7.0 0.7 %shared_first.1 = (bf16[1,256,1024]{2,1,0:T(8,128)(2,1)S(1)}, bf16[1,256,1024]{2,1,0:T(8,128)(2,1)S(1)}) custom-call(bf16[256,512]{1,0:T(8,128)(2,1)S(1)} %shared_up.1.hidden_ref, bf16[512,4096]{1,0:T(8,128)(2,1)S(1)} %copy-done.1), custom_call_target="tpu_custom_call" | custom-call | flops 536870912 | bytes 2097152 | tf_op jit(solution)/shard_map/shared_first/pallas_call | solution.py:300
  7.8 0.6 %collective-permute-start.4 = (bf16[1,256,1024]{2,1,0:T(8,128)(2,1)S(1)}, bf16[1,256,1024]{2,1,0:T(8,128)(2,1)S(1)}, u32[]{:S(2)}, u32[]{:S(2)}) collective-permute-start(bf16[1,256,1024]{2,1,0:T(8,128)(2,1)S(1)} %get-tuple-element.13), channel_id=1, source_target_pairs={{0,8},{8,0},{16,24},{24,16},{1,9},{9,1},{17,25},{25,17},{2,10},{10... | collective-permute-start | bytes 1572872 | tf_op jit(solution)/shard_map/ppermute | solution.py:312
  8.3 2.6 %collective-permute-start = (bf16[3,2,4096]{2,1,0:T(2,128)(2,1)S(1)}, bf16[3,2,4096]{2,1,0:T(2,128)(2,1)S(1)}, u32[]{:S(2)}, u32[]{:S(2)}) collective-permute-start(bf16[3,2,4096]{2,1,0:T(2,128)(2,1)S(1)} %get-tuple-element.12), channel_id=1, source_target_pairs={{0,1},{1,0},{2,3},{3,2},{4,5},{5,4},{6,7},{7,6},{8,9},{9,8},{10,11... | collective-permute-start | bytes 147464 | tf_op jit(solution)/shard_map/ppermute | solution.py:268
  10.9 2.3 %collective-permute-done.refs_1_ = bf16[3,2,4096]{2,1,0:T(2,128)(2,1)S(1)} collective-permute-done((bf16[3,2,4096]{2,1,0:T(2,128)(2,1)S(1)}, bf16[3,2,4096]{2,1,0:T(2,128)(2,1)S(1)}, u32[]{:S(2)}, u32[]{:S(2)}) %collective-permute-start) | collective-permute-done | bytes 49184 | tf_op jit(solution)/shard_map/ppermute | solution.py:268
  13.2 2.8 %collective-permute-start.2 = (bf16[2,2,4096]{2,1,0:T(2,128)(2,1)S(1)}, bf16[2,2,4096]{2,1,0:T(2,128)(2,1)S(1)}, u32[]{:S(2)}, u32[]{:S(2)}) collective-permute-start(bf16[2,2,4096]{2,1,0:T(2,128)(2,1)S(1)} %pack.3), channel_id=1, source_target_pairs={{0,4},{1,5},{2,6},{3,7},{4,0},{5,1},{6,2},{7,3},{8,14},{9,15},{10,... | collective-permute-start | bytes 98312 | tf_op jit(solution)/shard_map/ppermute | solution.py:274
  16.1 1.6 %collective-permute-start.1 = (bf16[2,2,4096]{2,1,0:T(2,128)(2,1)S(1)}, bf16[2,2,4096]{2,1,0:T(2,128)(2,1)S(1)}, u32[]{:S(2)}, u32[]{:S(2)}) collective-permute-start(bf16[2,2,4096]{2,1,0:T(2,128)(2,1)S(1)} %pack.2), channel_id=1, source_target_pairs={{0,2},{1,3},{2,0},{3,1},{4,6},{5,7},{6,4},{7,5},{8,10},{9,11},{10,... | collective-permute-start | bytes 98312 | tf_op jit(solution)/shard_map/ppermute | solution.py:275
  17.6 0.5 %collective-permute-done.2.refs_3_ = bf16[2,2,4096]{2,1,0:T(2,128)(2,1)S(1)} collective-permute-done((bf16[2,2,4096]{2,1,0:T(2,128)(2,1)S(1)}, bf16[2,2,4096]{2,1,0:T(2,128)(2,1)S(1)}, u32[]{:S(2)}, u32[]{:S(2)}) %collective-permute-start.2) | collective-permute-done | bytes 32800 | tf_op jit(solution)/shard_map/ppermute | solution.py:274
  18.2 0.0 collective-permute-start.3
  18.2 1.8 %collective-permute-done.1.refs_2_ = bf16[2,2,4096]{2,1,0:T(2,128)(2,1)S(1)} collective-permute-done((bf16[2,2,4096]{2,1,0:T(2,128)(2,1)S(1)}, bf16[2,2,4096]{2,1,0:T(2,128)(2,1)S(1)}, u32[]{:S(2)}, u32[]{:S(2)}) %collective-permute-start.1) | collective-permute-done | bytes 32800 | tf_op jit(solution)/shard_map/ppermute | solution.py:275
  20.0 0.0 collective-permute-done.3.refs_4_
  20.0 0.0 copy-done.3
  20.0 0.0 copy-done.4
  20.0 0.0 copy-done.2
  20.0 2.5 %routed.1.after_ref = bf16[32,2,1024]{2,1,0:T(2,128)(2,1)} custom-call(bf16[3,2,4096]{2,1,0:T(2,128)(2,1)S(1)} %get-tuple-element.11.refs_0_.after_ref, bf16[3,2,4096]{2,1,0:T(2,128)(2,1)S(1)} %collective-permute-done.refs_1_, bf16[2,2,4096]{2,1,0:T(2,128)(2,1)S(1)} %collective-permute-done.1.refs_2_, ...), custom_call_target="tpu_custom_call" | custom-call | flops 1073741824 | bytes 12582912 | tf_op jit(solution)/shard_map/routed/pallas_call | solution.py:327
  22.5 0.0 copy-start.8
  22.5 0.7 %shared_rest.1 = (bf16[256,1024]{1,0:T(8,128)(2,1)S(1)}, bf16[256,1024]{1,0:T(8,128)(2,1)S(1)}) custom-call(bf16[256,512]{1,0:T(8,128)(2,1)S(1)} %shared_up.1.hidden_ref, bf16[512,4096]{1,0:T(8,128)(2,1)S(1)} %copy-done.1, bf16[32,2,1024]{2,1,0:T(2,128)(2,1)} %routed.1.after_ref), custom_call_target="tpu_custom_call" | custom-call | flops 536870912 | bytes 2097152 | tf_op jit(solution)/shard_map/shared_rest/pallas_call | solution.py:341
  23.2 0.1 collective-permute-start.6
  23.3 0.0 collective-permute-done.4.a_ref
  23.3 0.1 add.1
  23.4 1.6 %collective-permute-start.5 = (bf16[256,1024]{1,0:T(8,128)(2,1)S(1)}, bf16[256,1024]{1,0:T(8,128)(2,1)S(1)}, u32[]{:S(2)}, u32[]{:S(2)}) collective-permute-start(bf16[256,1024]{1,0:T(8,128)(2,1)S(1)} %bitcast.3), channel_id=1, source_target_pairs={{0,16},{8,24},{16,0},{24,8},{1,17},{9,25},{17,1},{25,9},{2,18},{10... | collective-permute-start | bytes 1572872 | tf_op jit(solution)/shard_map/ppermute | solution.py:325
  25.0 4.8 %all-to-all-start = ((bf16[32,2,1024]{2,1,0:T(2,128)(2,1)}), bf16[32,2,1024]{2,1,0:T(2,128)(2,1)S(1)}, u32[]{:S(2)}, u32[]{:S(2)}) async-start(bf16[32,2,1024]{2,1,0:T(2,128)(2,1)} %routed.1.after_ref), calls=%async_computation | async-start | bytes 262144 | tf_op jit(solution)/shard_map/all_to_all | solution.py:337
  29.8 0.0 copy-done.8
  29.8 0.8 %mix.1.mix_ref = bf16[256,128]{1,0:T(8,128)(2,1)S(1)} custom-call(s32[8]{0:T(128)S(1)} %copy-done.9, s32[8]{0:T(128)S(1)} %copy-done.10, s32[8,256]{1,0:T(8,128)S(1)} %bitcast.5, f32[8,256]{1,0:T(8,128)S(1)} %bitcast.6, bf16[32,2,1024]{2,1,0:T(2,128)(2,1)} %routed.1.after_ref), custom_call_target="tpu_custom_call" | custom-call | tf_op jit(solution)/shard_map/mix/pallas_call | solution.py:353
  30.6 0.0 collective-permute-done.6.refs_0_
  30.6 8.4 %collective-permute-done.5.a_ref = bf16[256,1024]{1,0:T(8,128)(2,1)S(1)} collective-permute-done((bf16[256,1024]{1,0:T(8,128)(2,1)S(1)}, bf16[256,1024]{1,0:T(8,128)(2,1)S(1)}, u32[]{:S(2)}, u32[]{:S(2)}) %collective-permute-start.5) | collective-permute-done | bytes 524320 | tf_op jit(solution)/shard_map/ppermute | solution.py:325
  39.0 0.2 total.1.sum_ref
  39.2 1.0 %all-to-all-done.back_ref = bf16[32,2,1024]{2,1,0:T(2,128)(2,1)S(1)} async-done(((bf16[32,2,1024]{2,1,0:T(2,128)(2,1)}), bf16[32,2,1024]{2,1,0:T(2,128)(2,1)S(1)}, u32[]{:S(2)}, u32[]{:S(2)}) %all-to-all-start) | async-done | bytes 131104 | tf_op jit(solution)/shard_map/all_to_all | solution.py:337
  40.2 1.1 %combine.1 = bf16[256,1024]{1,0:T(8,128)(2,1)} custom-call(bf16[256,128]{1,0:T(8,128)(2,1)S(1)} %mix.1.mix_ref, bf16[32,2,1024]{2,1,0:T(2,128)(2,1)S(1)} %all-to-all-done.back_ref, f32[256,1024]{1,0:T(8,128)S(1)} %total.1.sum_ref), custom_call_target="tpu_custom_call" | custom-call | tf_op jit(solution)/shard_map/combine/pallas_call | solution.py:370
  (3 shorter events, 0.0 us)
Async XLA Ops:
  0.0 0.7 %copy-start.7 = (s32[256,8]{0,1:T(8,128)S(1)}, s32[256,8]{0,1:T(8,128)}, u32[]{:S(2)}) copy-start(s32[256,8]{0,1:T(8,128)} %param.12) | copy-start | bytes 24580
  0.0 0.7 %copy-start.9 = (s32[8]{0:T(128)S(1)}, s32[8]{0:T(128)}, u32[]{:S(2)}) copy-start(s32[8]{0:T(128)} %old_ref.3) | copy-start | bytes 100
  0.0 0.7 %copy-start.10 = (s32[8]{0:T(128)S(1)}, s32[8]{0:T(128)}, u32[]{:S(2)}) copy-start(s32[8]{0:T(128)} %new_ref.3) | copy-start | bytes 100
  0.0 1.6 %copy-start = (bf16[256,4096]{1,0:T(8,128)(2,1)S(1)}, bf16[256,4096]{1,0:T(8,128)(2,1)}, u32[]{:S(2)}) copy-start(bf16[256,4096]{1,0:T(8,128)(2,1)} %tok_ref.5) | copy-start | bytes 6291460
  0.0 2.9 %copy-start.6 = (bf16[4096,512]{1,0:T(8,128)(2,1)S(1)}, bf16[4096,512]{1,0:T(8,128)(2,1)}, u32[]{:S(2)}) copy-start(bf16[4096,512]{1,0:T(8,128)(2,1)} %gate_ref.1) | copy-start | bytes 12582916
  0.0 4.1 %copy-start.5 = (bf16[4096,512]{1,0:T(8,128)(2,1)S(1)}, bf16[4096,512]{1,0:T(8,128)(2,1)}, u32[]{:S(2)}) copy-start(bf16[4096,512]{1,0:T(8,128)(2,1)} %up_ref.1) | copy-start | bytes 12582916
  2.9 17.1 %copy-start.3 = (bf16[1,4096,512]{2,1,0:T(8,128)(2,1)S(1)}, bf16[1,4096,512]{2,1,0:T(8,128)(2,1)}, u32[]{:S(2)}) copy-start(bf16[1,4096,512]{2,1,0:T(8,128)(2,1)} %refs_6_.1) | copy-start | bytes 12582916
  2.9 17.1 %copy-start.4 = (bf16[1,512,4096]{2,1,0:T(8,128)(2,1)S(1)}, bf16[1,512,4096]{2,1,0:T(8,128)(2,1)}, u32[]{:S(2)}) copy-start(bf16[1,512,4096]{2,1,0:T(8,128)(2,1)} %refs_7_.1) | copy-start | bytes 12582916
  4.1 2.9 %copy-start.1 = (bf16[512,4096]{1,0:T(8,128)(2,1)S(1)}, bf16[512,4096]{1,0:T(8,128)(2,1)}, u32[]{:S(2)}) copy-start(bf16[512,4096]{1,0:T(8,128)(2,1)} %down_ref.3) | copy-start | bytes 12582916
  4.1 15.9 %copy-start.2 = (bf16[1,4096,512]{2,1,0:T(8,128)(2,1)S(1)}, bf16[1,4096,512]{2,1,0:T(8,128)(2,1)}, u32[]{:S(2)}) copy-start(bf16[1,4096,512]{2,1,0:T(8,128)(2,1)} %refs_5_.1) | copy-start | bytes 12582916
  7.8 15.5 %collective-permute-start.4 = (bf16[1,256,1024]{2,1,0:T(8,128)(2,1)S(1)}, bf16[1,256,1024]{2,1,0:T(8,128)(2,1)S(1)}, u32[]{:S(2)}, u32[]{:S(2)}) collective-permute-start(bf16[1,256,1024]{2,1,0:T(8,128)(2,1)S(1)} %get-tuple-element.13), channel_id=1, source_target_pairs={{0,8},{8,0},{16,24},{24,16},{1,9},{9,1},{17,25},{25,17},{2,10},{10... | collective-permute-start | bytes 1572872 | tf_op jit(solution)/shard_map/ppermute | solution.py:312
  8.3 4.9 %collective-permute-start = (bf16[3,2,4096]{2,1,0:T(2,128)(2,1)S(1)}, bf16[3,2,4096]{2,1,0:T(2,128)(2,1)S(1)}, u32[]{:S(2)}, u32[]{:S(2)}) collective-permute-start(bf16[3,2,4096]{2,1,0:T(2,128)(2,1)S(1)} %get-tuple-element.12), channel_id=1, source_target_pairs={{0,1},{1,0},{2,3},{3,2},{4,5},{5,4},{6,7},{7,6},{8,9},{9,8},{10,11... | collective-permute-start | bytes 147464 | tf_op jit(solution)/shard_map/ppermute | solution.py:268
  13.2 4.9 %collective-permute-start.2 = (bf16[2,2,4096]{2,1,0:T(2,128)(2,1)S(1)}, bf16[2,2,4096]{2,1,0:T(2,128)(2,1)S(1)}, u32[]{:S(2)}, u32[]{:S(2)}) collective-permute-start(bf16[2,2,4096]{2,1,0:T(2,128)(2,1)S(1)} %pack.3), channel_id=1, source_target_pairs={{0,4},{1,5},{2,6},{3,7},{4,0},{5,1},{6,2},{7,3},{8,14},{9,15},{10,... | collective-permute-start | bytes 98312 | tf_op jit(solution)/shard_map/ppermute | solution.py:274
  16.1 3.9 %collective-permute-start.1 = (bf16[2,2,4096]{2,1,0:T(2,128)(2,1)S(1)}, bf16[2,2,4096]{2,1,0:T(2,128)(2,1)S(1)}, u32[]{:S(2)}, u32[]{:S(2)}) collective-permute-start(bf16[2,2,4096]{2,1,0:T(2,128)(2,1)S(1)} %pack.2), channel_id=1, source_target_pairs={{0,2},{1,3},{2,0},{3,1},{4,6},{5,7},{6,4},{7,5},{8,10},{9,11},{10,... | collective-permute-start | bytes 98312 | tf_op jit(solution)/shard_map/ppermute | solution.py:275
  18.2 1.8 %collective-permute-start.3 = (bf16[2,2,4096]{2,1,0:T(2,128)(2,1)S(1)}, bf16[2,2,4096]{2,1,0:T(2,128)(2,1)S(1)}, u32[]{:S(2)}, u32[]{:S(2)}) collective-permute-start(bf16[2,2,4096]{2,1,0:T(2,128)(2,1)S(1)} %collective-permute-done.2.refs_3_), channel_id=1, source_target_pairs={{0,8},{8,0},{16,24},{24,16},{1,9},{9,1},{17,25},{25,17},{2,10},{10... | collective-permute-start | bytes 98312 | tf_op jit(solution)/shard_map/ppermute | solution.py:276
  22.5 7.3 %copy-start.8 = (f32[256,8]{0,1:T(8,128)S(1)}, f32[256,8]{0,1:T(8,128)}, u32[]{:S(2)}) copy-start(f32[256,8]{0,1:T(8,128)} %param.13) | copy-start | bytes 24580
  23.2 7.4 %collective-permute-start.6 = (bf16[256,1024]{1,0:T(8,128)(2,1)S(1)}, bf16[256,1024]{1,0:T(8,128)(2,1)S(1)}, u32[]{:S(2)}, u32[]{:S(2)}) collective-permute-start(bf16[256,1024]{1,0:T(8,128)(2,1)S(1)} %get-tuple-element.16), channel_id=1, source_target_pairs={{0,8},{8,0},{16,24},{24,16},{1,9},{9,1},{17,25},{25,17},{2,10},{10... | collective-permute-start | bytes 1572872 | tf_op jit(solution)/shard_map/ppermute | solution.py:350
  23.4 15.6 %collective-permute-start.5 = (bf16[256,1024]{1,0:T(8,128)(2,1)S(1)}, bf16[256,1024]{1,0:T(8,128)(2,1)S(1)}, u32[]{:S(2)}, u32[]{:S(2)}) collective-permute-start(bf16[256,1024]{1,0:T(8,128)(2,1)S(1)} %bitcast.3), channel_id=1, source_target_pairs={{0,16},{8,24},{16,0},{24,8},{1,17},{9,25},{17,1},{25,9},{2,18},{10... | collective-permute-start | bytes 1572872 | tf_op jit(solution)/shard_map/ppermute | solution.py:325
  25.0 15.2 %all-to-all-start = ((bf16[32,2,1024]{2,1,0:T(2,128)(2,1)}), bf16[32,2,1024]{2,1,0:T(2,128)(2,1)S(1)}, u32[]{:S(2)}, u32[]{:S(2)}) async-start(bf16[32,2,1024]{2,1,0:T(2,128)(2,1)} %routed.1.after_ref), calls=%async_computation | async-start | bytes 262144 | tf_op jit(solution)/shard_map/all_to_all | solution.py:337

commit v4 on v3

--- a/solution.py
+++ b/solution.py
@@ -28,7 +28,7 @@
     tok = ids.shape[1]
     rows = count * span * ranks
     row = lax.broadcasted_iota(jnp.int32, (rows, 1), 0)
-    block, rank = row // (span * ranks), row % ranks
+    block, rank = row // ranks % count, row % ranks
     plan = jnp.full((rows, 1), -1, jnp.int32)
     for index in range(count):
         slot = slot_of(index)
@@ -162,7 +162,8 @@
 def routed_kernel(parts, places, *refs):
     arrays, (gate_ref, up_ref, down_ref, out_ref, rows_ref) = refs[:-5], refs[-5:]
     width = out_ref.shape[2]
-    quarter = len(places) // 4
+    slots = len(places)
+    quarter = slots // 4
     me = lax.axis_index("expert")
     core = lax.axis_index("dp") % 2
     offsets = (0, quarter, 2 * quarter + quarter * core, 3 * quarter - quarter * core)
@@ -174,7 +175,7 @@
         value = dot(hidden, down_ref[0, :, part * width : (part + 1) * width]).astype(BF)
         for place in range(len(places)):
             sender = me ^ (place % quarter + offsets[place // quarter])
-            out_ref[sender * parts + part] = value[place * CAP : (place + 1) * CAP, :]
+            out_ref[part * slots + sender] = value[place * CAP : (place + 1) * CAP, :]
 
 
 def cost(flops, size):
@@ -335,7 +336,7 @@
         compiler_params=params(20),
     )(*arrays, gate_weight, up_weight, down_weight)
     back = lax.all_to_all(
-        routed, ("expert", "dp"), split_axis=0, concat_axis=0, tiled=True
+        routed, ("dp", "expert"), split_axis=0, concat_axis=0, tiled=True
     )
 
     send_rest, keep_rest = pl.pallas_call(

time: 41.5 us -> 41.4 us (level)
  no operation moved by 1% of the time
where the time goes in v4:
time: 41.4 us; the launch traced here: 41.2 us
  starting transfers between devices  14 us (34%)
  waiting for transfers between devices  13.9 us (34%)
  Pallas kernels  9.73 us (24%)
  local copies, waits for them, and re-layouts  3.4 us (8%)
    ppermute x1, waiting for transfers between devices, local(): sums.append(lax.ppermute(chip_sum[k - 1], 'dp', moves))  8.38 us
    all_to_all x1, starting transfers between devices, local(): lax.all_to_all(routed, ('dp', 'expert'), split_axis=0, concat_axis=0, til...  4.82 us
    unnamed x22, local copies, waits for them, and re-layouts  3.4 us
    ppermute x1, starting transfers between devices, local(): far = lax.ppermute(far, ('dp', 'expert'), across)  2.82 us
    ppermute x1, starting transfers between devices, local(): lax.ppermute(moving, 'expert', [(e, e ^ bit) for e in range(slots)])  2.58 us
    pallas_call x1, Pallas kernels, local(): pl.pallas_call(functools.partial(routed_kernel, parts, places), out_shape...  2.49 us
    ppermute x1, waiting for transfers between devices, local(): lax.ppermute(moving, 'expert', [(e, e ^ bit) for e in range(slots)])  2.33 us
    ppermute x1, waiting for transfers between devices, local(): lax.ppermute(near, 'expert', [(e, e ^ quarter) for e in range(slots)])  1.79 us
  transfers between devices with their start and end apart: 8, of which 5 were waited for; matrix products, arithmetic and copies ran while one was open for 0% of the time, Pallas kernels for 10%

profile of v4, /device:TPU:0, one launch (start us, length us, event | category | flops | bytes accessed | tf_op | source)
XLA Modules:
  0.0 41.2 jit_solution(15951870745419462375)
XLA Ops:
  0.0 0.0 copy-start.7
  0.0 0.0 copy-start.9
  0.0 0.0 copy-start.10
  0.0 0.0 copy-start
  0.0 0.0 copy-start.6
  0.0 0.0 copy-start.5
  0.0 0.7 %copy-done.7 = s32[256,8]{0,1:T(8,128)S(1)} copy-done((s32[256,8]{0,1:T(8,128)S(1)}, s32[256,8]{0,1:T(8,128)}, u32[]{:S(2)}) %copy-start.7) | copy-done | bytes 8216
  0.7 0.0 copy-done.9
  0.7 0.0 copy-done.10
  0.7 0.7 %select.1.chosen_ref = bf16[12,256]{1,0:T(8,128)(2,1)S(1)} custom-call(s32[8]{0:T(128)S(1)} %copy-done.9, s32[8]{0:T(128)S(1)} %copy-done.10, s32[8,256]{1,0:T(8,128)S(1)} %bitcast.4, f32[8,128]{1,0:T(8,128)S(1)} %ready.1.after_ref), custom_call_target="tpu_custom_call" | custom-call | flops 2097152 | bytes 2097152 | tf_op jit(solution)/shard_map/select/pallas_call | solution.py:234
  1.4 0.2 copy-done
  1.6 0.4 pick.1
  2.0 0.8 %copy-done.6 = bf16[4096,512]{1,0:T(8,128)(2,1)S(1)} copy-done((bf16[4096,512]{1,0:T(8,128)(2,1)S(1)}, bf16[4096,512]{1,0:T(8,128)(2,1)}, u32[]{:S(2)}) %copy-start.6) | copy-done | bytes 4194328
  2.9 0.0 copy-start.3
  2.9 0.0 copy-start.4
  2.9 1.2 %shared_gate.1.value_ref = f32[256,512]{1,0:T(8,128)S(1)} custom-call(bf16[256,4096]{1,0:T(8,128)(2,1)S(1)} %copy-done, bf16[4096,512]{1,0:T(8,128)(2,1)S(1)} %copy-done.6, bf16[3,2,4096]{2,1,0:T(2,128)(2,1)S(1)} %get-tuple-element.11.refs_0_.after_ref), custom_call_target="tpu_custom_call" | custom-call | flops 1073741824 | bytes 4194304 | tf_op jit(solution)/shard_map/shared_gate/pallas_call | solution.py:283
  4.1 0.0 copy-done.5
  4.1 0.0 copy-start.1
  4.1 0.0 copy-start.2
  4.1 1.3 %shared_up.1.hidden_ref = bf16[256,512]{1,0:T(8,128)(2,1)S(1)} custom-call(bf16[256,4096]{1,0:T(8,128)(2,1)S(1)} %copy-done, bf16[4096,512]{1,0:T(8,128)(2,1)S(1)} %copy-done.5, f32[256,512]{1,0:T(8,128)S(1)} %shared_gate.1.value_ref), custom_call_target="tpu_custom_call" | custom-call | flops 1073741824 | bytes 4194304 | tf_op jit(solution)/shard_map/shared_up/pallas_call | solution.py:292
  5.4 1.6 %copy-done.1 = bf16[512,4096]{1,0:T(8,128)(2,1)S(1)} copy-done((bf16[512,4096]{1,0:T(8,128)(2,1)S(1)}, bf16[512,4096]{1,0:T(8,128)(2,1)}, u32[]{:S(2)}) %copy-start.1) | copy-done | bytes 4194328
  7.0 0.7 %shared_first.1 = (bf16[1,256,1024]{2,1,0:T(8,128)(2,1)S(1)}, bf16[1,256,1024]{2,1,0:T(8,128)(2,1)S(1)}) custom-call(bf16[256,512]{1,0:T(8,128)(2,1)S(1)} %shared_up.1.hidden_ref, bf16[512,4096]{1,0:T(8,128)(2,1)S(1)} %copy-done.1), custom_call_target="tpu_custom_call" | custom-call | flops 536870912 | bytes 2097152 | tf_op jit(solution)/shard_map/shared_first/pallas_call | solution.py:301
  7.8 0.6 %collective-permute-start.4 = (bf16[1,256,1024]{2,1,0:T(8,128)(2,1)S(1)}, bf16[1,256,1024]{2,1,0:T(8,128)(2,1)S(1)}, u32[]{:S(2)}, u32[]{:S(2)}) collective-permute-start(bf16[1,256,1024]{2,1,0:T(8,128)(2,1)S(1)} %get-tuple-element.13), channel_id=1, source_target_pairs={{0,8},{8,0},{16,24},{24,16},{1,9},{9,1},{17,25},{25,17},{2,10},{10... | collective-permute-start | bytes 1572872 | tf_op jit(solution)/shard_map/ppermute | solution.py:313
  8.3 2.6 %collective-permute-start = (bf16[3,2,4096]{2,1,0:T(2,128)(2,1)S(1)}, bf16[3,2,4096]{2,1,0:T(2,128)(2,1)S(1)}, u32[]{:S(2)}, u32[]{:S(2)}) collective-permute-start(bf16[3,2,4096]{2,1,0:T(2,128)(2,1)S(1)} %get-tuple-element.12), channel_id=1, source_target_pairs={{0,1},{1,0},{2,3},{3,2},{4,5},{5,4},{6,7},{7,6},{8,9},{9,8},{10,11... | collective-permute-start | bytes 147464 | tf_op jit(solution)/shard_map/ppermute | solution.py:269
  10.9 2.3 %collective-permute-done.refs_1_ = bf16[3,2,4096]{2,1,0:T(2,128)(2,1)S(1)} collective-permute-done((bf16[3,2,4096]{2,1,0:T(2,128)(2,1)S(1)}, bf16[3,2,4096]{2,1,0:T(2,128)(2,1)S(1)}, u32[]{:S(2)}, u32[]{:S(2)}) %collective-permute-start) | collective-permute-done | bytes 49184 | tf_op jit(solution)/shard_map/ppermute | solution.py:269
  13.2 2.8 %collective-permute-start.2 = (bf16[2,2,4096]{2,1,0:T(2,128)(2,1)S(1)}, bf16[2,2,4096]{2,1,0:T(2,128)(2,1)S(1)}, u32[]{:S(2)}, u32[]{:S(2)}) collective-permute-start(bf16[2,2,4096]{2,1,0:T(2,128)(2,1)S(1)} %pack.3), channel_id=1, source_target_pairs={{0,4},{1,5},{2,6},{3,7},{4,0},{5,1},{6,2},{7,3},{8,14},{9,15},{10,... | collective-permute-start | bytes 98312 | tf_op jit(solution)/shard_map/ppermute | solution.py:275
  16.1 1.6 %collective-permute-start.1 = (bf16[2,2,4096]{2,1,0:T(2,128)(2,1)S(1)}, bf16[2,2,4096]{2,1,0:T(2,128)(2,1)S(1)}, u32[]{:S(2)}, u32[]{:S(2)}) collective-permute-start(bf16[2,2,4096]{2,1,0:T(2,128)(2,1)S(1)} %pack.2), channel_id=1, source_target_pairs={{0,2},{1,3},{2,0},{3,1},{4,6},{5,7},{6,4},{7,5},{8,10},{9,11},{10,... | collective-permute-start | bytes 98312 | tf_op jit(solution)/shard_map/ppermute | solution.py:276
  17.6 0.5 %collective-permute-done.2.refs_3_ = bf16[2,2,4096]{2,1,0:T(2,128)(2,1)S(1)} collective-permute-done((bf16[2,2,4096]{2,1,0:T(2,128)(2,1)S(1)}, bf16[2,2,4096]{2,1,0:T(2,128)(2,1)S(1)}, u32[]{:S(2)}, u32[]{:S(2)}) %collective-permute-start.2) | collective-permute-done | bytes 32800 | tf_op jit(solution)/shard_map/ppermute | solution.py:275
  18.2 0.0 collective-permute-start.3
  18.2 1.8 %collective-permute-done.1.refs_2_ = bf16[2,2,4096]{2,1,0:T(2,128)(2,1)S(1)} collective-permute-done((bf16[2,2,4096]{2,1,0:T(2,128)(2,1)S(1)}, bf16[2,2,4096]{2,1,0:T(2,128)(2,1)S(1)}, u32[]{:S(2)}, u32[]{:S(2)}) %collective-permute-start.1) | collective-permute-done | bytes 32800 | tf_op jit(solution)/shard_map/ppermute | solution.py:276
  20.0 0.0 collective-permute-done.3.refs_4_
  20.0 0.0 copy-done.3
  20.0 0.0 copy-done.4
  20.0 0.0 copy-done.2
  20.0 2.5 %routed.1.after_ref = bf16[32,2,1024]{2,1,0:T(2,128)(2,1)} custom-call(bf16[3,2,4096]{2,1,0:T(2,128)(2,1)S(1)} %get-tuple-element.11.refs_0_.after_ref, bf16[3,2,4096]{2,1,0:T(2,128)(2,1)S(1)} %collective-permute-done.refs_1_, bf16[2,2,4096]{2,1,0:T(2,128)(2,1)S(1)} %collective-permute-done.1.refs_2_, ...), custom_call_target="tpu_custom_call" | custom-call | flops 1073741824 | bytes 12582912 | tf_op jit(solution)/shard_map/routed/pallas_call | solution.py:328
  22.5 0.0 copy-start.8
  22.5 0.7 %shared_rest.1 = (bf16[256,1024]{1,0:T(8,128)(2,1)S(1)}, bf16[256,1024]{1,0:T(8,128)(2,1)S(1)}) custom-call(bf16[256,512]{1,0:T(8,128)(2,1)S(1)} %shared_up.1.hidden_ref, bf16[512,4096]{1,0:T(8,128)(2,1)S(1)} %copy-done.1, bf16[32,2,1024]{2,1,0:T(2,128)(2,1)} %routed.1.after_ref), custom_call_target="tpu_custom_call" | custom-call | flops 536870912 | bytes 2097152 | tf_op jit(solution)/shard_map/shared_rest/pallas_call | solution.py:342
  23.2 0.1 collective-permute-start.6
  23.3 0.0 collective-permute-done.4.a_ref
  23.3 0.1 add.1
  23.4 1.6 %collective-permute-start.5 = (bf16[256,1024]{1,0:T(8,128)(2,1)S(1)}, bf16[256,1024]{1,0:T(8,128)(2,1)S(1)}, u32[]{:S(2)}, u32[]{:S(2)}) collective-permute-start(bf16[256,1024]{1,0:T(8,128)(2,1)S(1)} %bitcast.3), channel_id=1, source_target_pairs={{0,16},{8,24},{16,0},{24,8},{1,17},{9,25},{17,1},{25,9},{2,18},{10... | collective-permute-start | bytes 1572872 | tf_op jit(solution)/shard_map/ppermute | solution.py:326
  25.0 4.8 %all-to-all-start = ((bf16[32,2,1024]{2,1,0:T(2,128)(2,1)}), bf16[32,2,1024]{2,1,0:T(2,128)(2,1)S(1)}, u32[]{:S(2)}, u32[]{:S(2)}) async-start(bf16[32,2,1024]{2,1,0:T(2,128)(2,1)} %routed.1.after_ref), calls=%async_computation | async-start | bytes 262144 | tf_op jit(solution)/shard_map/all_to_all | solution.py:338
  29.8 0.0 copy-done.8
  29.8 0.8 %mix.1.mix_ref = bf16[256,128]{1,0:T(8,128)(2,1)S(1)} custom-call(s32[8]{0:T(128)S(1)} %copy-done.9, s32[8]{0:T(128)S(1)} %copy-done.10, s32[8,256]{1,0:T(8,128)S(1)} %bitcast.5, f32[8,256]{1,0:T(8,128)S(1)} %bitcast.6, bf16[32,2,1024]{2,1,0:T(2,128)(2,1)} %routed.1.after_ref), custom_call_target="tpu_custom_call" | custom-call | tf_op jit(solution)/shard_map/mix/pallas_call | solution.py:354
  30.6 0.0 collective-permute-done.6.refs_0_
  30.7 8.4 %collective-permute-done.5.a_ref = bf16[256,1024]{1,0:T(8,128)(2,1)S(1)} collective-permute-done((bf16[256,1024]{1,0:T(8,128)(2,1)S(1)}, bf16[256,1024]{1,0:T(8,128)(2,1)S(1)}, u32[]{:S(2)}, u32[]{:S(2)}) %collective-permute-start.5) | collective-permute-done | bytes 524320 | tf_op jit(solution)/shard_map/ppermute | solution.py:326
  39.0 0.2 total.1.sum_ref
  39.2 0.9 %all-to-all-done.back_ref = bf16[32,2,1024]{2,1,0:T(2,128)(2,1)S(1)} async-done(((bf16[32,2,1024]{2,1,0:T(2,128)(2,1)}), bf16[32,2,1024]{2,1,0:T(2,128)(2,1)S(1)}, u32[]{:S(2)}, u32[]{:S(2)}) %all-to-all-start) | async-done | bytes 131104 | tf_op jit(solution)/shard_map/all_to_all | solution.py:338
  40.1 1.1 %combine.1 = bf16[256,1024]{1,0:T(8,128)(2,1)} custom-call(bf16[256,128]{1,0:T(8,128)(2,1)S(1)} %mix.1.mix_ref, bf16[32,2,1024]{2,1,0:T(2,128)(2,1)S(1)} %all-to-all-done.back_ref, f32[256,1024]{1,0:T(8,128)S(1)} %total.1.sum_ref), custom_call_target="tpu_custom_call" | custom-call | tf_op jit(solution)/shard_map/combine/pallas_call | solution.py:371
  (3 shorter events, 0.0 us)
Async XLA Ops:
  0.0 0.7 %copy-start.7 = (s32[256,8]{0,1:T(8,128)S(1)}, s32[256,8]{0,1:T(8,128)}, u32[]{:S(2)}) copy-start(s32[256,8]{0,1:T(8,128)} %param.12) | copy-start | bytes 24580
  0.0 0.7 %copy-start.9 = (s32[8]{0:T(128)S(1)}, s32[8]{0:T(128)}, u32[]{:S(2)}) copy-start(s32[8]{0:T(128)} %old_ref.3) | copy-start | bytes 100
  0.0 0.7 %copy-start.10 = (s32[8]{0:T(128)S(1)}, s32[8]{0:T(128)}, u32[]{:S(2)}) copy-start(s32[8]{0:T(128)} %new_ref.3) | copy-start | bytes 100
  0.0 1.6 %copy-start = (bf16[256,4096]{1,0:T(8,128)(2,1)S(1)}, bf16[256,4096]{1,0:T(8,128)(2,1)}, u32[]{:S(2)}) copy-start(bf16[256,4096]{1,0:T(8,128)(2,1)} %tok_ref.5) | copy-start | bytes 6291460
  0.0 2.9 %copy-start.6 = (bf16[4096,512]{1,0:T(8,128)(2,1)S(1)}, bf16[4096,512]{1,0:T(8,128)(2,1)}, u32[]{:S(2)}) copy-start(bf16[4096,512]{1,0:T(8,128)(2,1)} %gate_ref.1) | copy-start | bytes 12582916
  0.0 4.1 %copy-start.5 = (bf16[4096,512]{1,0:T(8,128)(2,1)S(1)}, bf16[4096,512]{1,0:T(8,128)(2,1)}, u32[]{:S(2)}) copy-start(bf16[4096,512]{1,0:T(8,128)(2,1)} %up_ref.1) | copy-start | bytes 12582916
  2.9 17.1 %copy-start.3 = (bf16[1,4096,512]{2,1,0:T(8,128)(2,1)S(1)}, bf16[1,4096,512]{2,1,0:T(8,128)(2,1)}, u32[]{:S(2)}) copy-start(bf16[1,4096,512]{2,1,0:T(8,128)(2,1)} %refs_6_.1) | copy-start | bytes 12582916
  2.9 17.1 %copy-start.4 = (bf16[1,512,4096]{2,1,0:T(8,128)(2,1)S(1)}, bf16[1,512,4096]{2,1,0:T(8,128)(2,1)}, u32[]{:S(2)}) copy-start(bf16[1,512,4096]{2,1,0:T(8,128)(2,1)} %refs_7_.1) | copy-start | bytes 12582916
  4.1 2.9 %copy-start.1 = (bf16[512,4096]{1,0:T(8,128)(2,1)S(1)}, bf16[512,4096]{1,0:T(8,128)(2,1)}, u32[]{:S(2)}) copy-start(bf16[512,4096]{1,0:T(8,128)(2,1)} %down_ref.3) | copy-start | bytes 12582916
  4.1 15.9 %copy-start.2 = (bf16[1,4096,512]{2,1,0:T(8,128)(2,1)S(1)}, bf16[1,4096,512]{2,1,0:T(8,128)(2,1)}, u32[]{:S(2)}) copy-start(bf16[1,4096,512]{2,1,0:T(8,128)(2,1)} %refs_5_.1) | copy-start | bytes 12582916
  7.8 15.5 %collective-permute-start.4 = (bf16[1,256,1024]{2,1,0:T(8,128)(2,1)S(1)}, bf16[1,256,1024]{2,1,0:T(8,128)(2,1)S(1)}, u32[]{:S(2)}, u32[]{:S(2)}) collective-permute-start(bf16[1,256,1024]{2,1,0:T(8,128)(2,1)S(1)} %get-tuple-element.13), channel_id=1, source_target_pairs={{0,8},{8,0},{16,24},{24,16},{1,9},{9,1},{17,25},{25,17},{2,10},{10... | collective-permute-start | bytes 1572872 | tf_op jit(solution)/shard_map/ppermute | solution.py:313
  8.3 4.9 %collective-permute-start = (bf16[3,2,4096]{2,1,0:T(2,128)(2,1)S(1)}, bf16[3,2,4096]{2,1,0:T(2,128)(2,1)S(1)}, u32[]{:S(2)}, u32[]{:S(2)}) collective-permute-start(bf16[3,2,4096]{2,1,0:T(2,128)(2,1)S(1)} %get-tuple-element.12), channel_id=1, source_target_pairs={{0,1},{1,0},{2,3},{3,2},{4,5},{5,4},{6,7},{7,6},{8,9},{9,8},{10,11... | collective-permute-start | bytes 147464 | tf_op jit(solution)/shard_map/ppermute | solution.py:269
  13.2 4.9 %collective-permute-start.2 = (bf16[2,2,4096]{2,1,0:T(2,128)(2,1)S(1)}, bf16[2,2,4096]{2,1,0:T(2,128)(2,1)S(1)}, u32[]{:S(2)}, u32[]{:S(2)}) collective-permute-start(bf16[2,2,4096]{2,1,0:T(2,128)(2,1)S(1)} %pack.3), channel_id=1, source_target_pairs={{0,4},{1,5},{2,6},{3,7},{4,0},{5,1},{6,2},{7,3},{8,14},{9,15},{10,... | collective-permute-start | bytes 98312 | tf_op jit(solution)/shard_map/ppermute | solution.py:275
  16.1 3.9 %collective-permute-start.1 = (bf16[2,2,4096]{2,1,0:T(2,128)(2,1)S(1)}, bf16[2,2,4096]{2,1,0:T(2,128)(2,1)S(1)}, u32[]{:S(2)}, u32[]{:S(2)}) collective-permute-start(bf16[2,2,4096]{2,1,0:T(2,128)(2,1)S(1)} %pack.2), channel_id=1, source_target_pairs={{0,2},{1,3},{2,0},{3,1},{4,6},{5,7},{6,4},{7,5},{8,10},{9,11},{10,... | collective-permute-start | bytes 98312 | tf_op jit(solution)/shard_map/ppermute | solution.py:276
  18.2 1.8 %collective-permute-start.3 = (bf16[2,2,4096]{2,1,0:T(2,128)(2,1)S(1)}, bf16[2,2,4096]{2,1,0:T(2,128)(2,1)S(1)}, u32[]{:S(2)}, u32[]{:S(2)}) collective-permute-start(bf16[2,2,4096]{2,1,0:T(2,128)(2,1)S(1)} %collective-permute-done.2.refs_3_), channel_id=1, source_target_pairs={{0,8},{8,0},{16,24},{24,16},{1,9},{9,1},{17,25},{25,17},{2,10},{10... | collective-permute-start | bytes 98312 | tf_op jit(solution)/shard_map/ppermute | solution.py:277
  22.5 7.3 %copy-start.8 = (f32[256,8]{0,1:T(8,128)S(1)}, f32[256,8]{0,1:T(8,128)}, u32[]{:S(2)}) copy-start(f32[256,8]{0,1:T(8,128)} %param.13) | copy-start | bytes 24580
  23.2 7.4 %collective-permute-start.6 = (bf16[256,1024]{1,0:T(8,128)(2,1)S(1)}, bf16[256,1024]{1,0:T(8,128)(2,1)S(1)}, u32[]{:S(2)}, u32[]{:S(2)}) collective-permute-start(bf16[256,1024]{1,0:T(8,128)(2,1)S(1)} %get-tuple-element.16), channel_id=1, source_target_pairs={{0,8},{8,0},{16,24},{24,16},{1,9},{9,1},{17,25},{25,17},{2,10},{10... | collective-permute-start | bytes 1572872 | tf_op jit(solution)/shard_map/ppermute | solution.py:351
  23.4 15.6 %collective-permute-start.5 = (bf16[256,1024]{1,0:T(8,128)(2,1)S(1)}, bf16[256,1024]{1,0:T(8,128)(2,1)S(1)}, u32[]{:S(2)}, u32[]{:S(2)}) collective-permute-start(bf16[256,1024]{1,0:T(8,128)(2,1)S(1)} %bitcast.3), channel_id=1, source_target_pairs={{0,16},{8,24},{16,0},{24,8},{1,17},{9,25},{17,1},{25,9},{2,18},{10... | collective-permute-start | bytes 1572872 | tf_op jit(solution)/shard_map/ppermute | solution.py:326
  25.0 15.1 %all-to-all-start = ((bf16[32,2,1024]{2,1,0:T(2,128)(2,1)}), bf16[32,2,1024]{2,1,0:T(2,128)(2,1)S(1)}, u32[]{:S(2)}, u32[]{:S(2)}) async-start(bf16[32,2,1024]{2,1,0:T(2,128)(2,1)} %routed.1.after_ref), calls=%async_computation | async-start | bytes 262144 | tf_op jit(solution)/shard_map/all_to_all | solution.py:338

commit v5 on v4

--- a/solution.py
+++ b/solution.py
@@ -91,7 +91,7 @@
     out_ref[...] = (a_ref[...].astype(F32) + b_ref[...].astype(F32)).astype(BF)
 
 
-def mix_kernel(slots, parts, old_ref, new_ref, ids_ref, weight_ref, after_ref, mix_ref):
+def mix_kernel(slots, parts, old_ref, new_ref, ids_ref, weight_ref, mix_ref):
     chosen, scale = route_rows(
         ids_ref[...], weight_ref[...], old_ref, new_ref, lambda k: k, parts, slots, CAP, slots
     )
@@ -150,7 +150,7 @@
             target[k - 1] = dot(hidden_ref[...], block).astype(BF)
 
 
-def shared_rest_kernel(hidden_ref, down_ref, after_ref, send_ref, keep_ref):
+def shared_rest_kernel(hidden_ref, down_ref, send_ref, keep_ref):
     width = send_ref.shape[1]
     me = lax.axis_index("dp")
     chip, core = me // 2, me % 2
@@ -342,23 +342,23 @@
     send_rest, keep_rest = pl.pallas_call(
         shared_rest_kernel,
         out_shape=(rows, rows),
-        in_specs=[spec(VMEM)] * 2 + [spec(ANY)],
+        in_specs=[spec(VMEM)] * 2,
         out_specs=(spec(VMEM),) * 2,
         name="shared_rest",
         cost_estimate=cost(4 * tok * hidden_width * width, 4 * hidden_width * width),
         compiler_params=params(12),
-    )(hidden, shared_down, routed)
+    )(hidden, shared_down)
     sums += [keep_rest, lax.ppermute(send_rest, "dp", pairs)]
 
     blocks = slots * parts
     mix = pl.pallas_call(
         functools.partial(mix_kernel, slots, parts),
         out_shape=jax.ShapeDtypeStruct((tok, 2 * blocks * CAP), BF),
-        in_specs=[spec(SMEM), spec(SMEM), spec(VMEM), spec(VMEM), spec(ANY)],
+        in_specs=[spec(SMEM), spec(SMEM), spec(VMEM), spec(VMEM)],
         out_specs=spec(VMEM),
         name="mix",
         compiler_params=params(8),
-    )(old_plan, new_plan, ids, weight, routed)
+    )(old_plan, new_plan, ids, weight)
     total = pl.pallas_call(
         total_kernel,
         out_shape=jax.ShapeDtypeStruct((tok, width), F32),

time: 41.4 us -> 39.3 us (0.949)
  waiting for transfers between devices: 13.9 us -> 12.4 us
  local copies, waits for them, and re-layouts: 3.4 us -> 2.91 us
    ppermute x1, waiting for transfers between devices: 8.38 us -> 0.01 us  [local(): sums.append(lax.ppermute(chip_sum[k - 1], 'dp', moves))]
    all_to_all x1, waiting for transfers between devices: 0.87 us -> 6.77 us  [local(): lax.all_to_all(routed, ('dp', 'expert'), split_axis=0, concat_axis=0, til...]
    ppermute x1, starting transfers between devices: 1.56 us -> 2.91 us  [local(): sums.append(lax.ppermute(chip_sum[k - 1], 'dp', moves))]
    ppermute x1, starting transfers between devices: 2.58 us -> 1.52 us  [local(): lax.ppermute(moving, 'expert', [(e, e ^ bit) for e in range(slots)])]
    ppermute x1, waiting for transfers between devices: 0.01 us -> 0.72 us  [local(): partner = lax.ppermute(send, 'dp', pairs)]
    unnamed x22, local copies, waits for them, and re-layouts: 3.4 us -> 2.91 us
  transfers between devices with their start and end apart: 8 -> 8, of which waited for: 5 -> 5; matrix products, arithmetic and copies ran while one was open for 0% -> 0% of each run, Pallas kernels for 10% -> 11%
where the time goes in v5:
time: 39.3 us; the launch traced here: 39.1 us
  starting transfers between devices  13.9 us (35%)
  waiting for transfers between devices  12.4 us (32%)
  Pallas kernels  9.72 us (25%)
  local copies, waits for them, and re-layouts  2.91 us (7%)
    all_to_all x1, waiting for transfers between devices, local(): lax.all_to_all(routed, ('dp', 'expert'), split_axis=0, concat_axis=0, til...  6.77 us
    all_to_all x1, starting transfers between devices, local(): lax.all_to_all(routed, ('dp', 'expert'), split_axis=0, concat_axis=0, til...  4.66 us
    ppermute x1, starting transfers between devices, local(): sums.append(lax.ppermute(chip_sum[k - 1], 'dp', moves))  2.91 us
    unnamed x22, local copies, waits for them, and re-layouts  2.91 us
    ppermute x1, starting transfers between devices, local(): far = lax.ppermute(far, ('dp', 'expert'), across)  2.59 us
    ppermute x1, waiting for transfers between devices, local(): lax.ppermute(moving, 'expert', [(e, e ^ bit) for e in range(slots)])  2.57 us
    pallas_call x1, Pallas kernels, local(): pl.pallas_call(functools.partial(routed_kernel, parts, places), out_shape...  2.49 us
    ppermute x1, waiting for transfers between devices, local(): lax.ppermute(near, 'expert', [(e, e ^ quarter) for e in range(slots)])  1.69 us
  transfers between devices with their start and end apart: 8, of which 5 were waited for; matrix products, arithmetic and copies ran while one was open for 0% of the time, Pallas kernels for 11%

profile of v5, /device:TPU:0, one launch (start us, length us, event | category | flops | bytes accessed | tf_op | source)
XLA Modules:
  0.0 39.1 jit_solution(18158967360943043837)
XLA Ops:
  0.0 0.0 copy-start.7
  0.0 0.0 copy-start.9
  0.0 0.0 copy-start.10
  0.0 0.0 copy-start
  0.0 0.0 copy-start.6
  0.0 0.7 %copy-done.7 = s32[256,8]{0,1:T(8,128)S(1)} copy-done((s32[256,8]{0,1:T(8,128)S(1)}, s32[256,8]{0,1:T(8,128)}, u32[]{:S(2)}) %copy-start.7) | copy-done | bytes 8216
  0.7 0.0 copy-done.9
  0.7 0.0 copy-done.10
  0.7 0.7 %select.1.chosen_ref = bf16[12,256]{1,0:T(8,128)(2,1)S(1)} custom-call(s32[8]{0:T(128)S(1)} %copy-done.9, s32[8]{0:T(128)S(1)} %copy-done.10, s32[8,256]{1,0:T(8,128)S(1)} %bitcast.4, f32[8,128]{1,0:T(8,128)S(1)} %ready.1.after_ref), custom_call_target="tpu_custom_call" | custom-call | flops 2097152 | bytes 2097152 | tf_op jit(solution)/shard_map/select/pallas_call | solution.py:234
  1.4 0.2 copy-done
  1.6 0.0 copy-start.5
  1.6 0.4 pick.1
  2.0 0.8 %copy-done.6 = bf16[4096,512]{1,0:T(8,128)(2,1)S(1)} copy-done((bf16[4096,512]{1,0:T(8,128)(2,1)S(1)}, bf16[4096,512]{1,0:T(8,128)(2,1)}, u32[]{:S(2)}) %copy-start.6) | copy-done | bytes 4194328
  2.9 1.2 %shared_gate.1.value_ref = f32[256,512]{1,0:T(8,128)S(1)} custom-call(bf16[256,4096]{1,0:T(8,128)(2,1)S(1)} %copy-done, bf16[4096,512]{1,0:T(8,128)(2,1)S(1)} %copy-done.6, bf16[3,2,4096]{2,1,0:T(2,128)(2,1)S(1)} %get-tuple-element.11.refs_0_.after_ref), custom_call_target="tpu_custom_call" | custom-call | flops 1073741824 | bytes 4194304 | tf_op jit(solution)/shard_map/shared_gate/pallas_call | solution.py:283
  4.1 0.2 copy-done.5
  4.3 0.0 copy-start.1
  4.3 0.0 copy-start.4
  4.3 1.2 %shared_up.1.hidden_ref = bf16[256,512]{1,0:T(8,128)(2,1)S(1)} custom-call(bf16[256,4096]{1,0:T(8,128)(2,1)S(1)} %copy-done, bf16[4096,512]{1,0:T(8,128)(2,1)S(1)} %copy-done.5, f32[256,512]{1,0:T(8,128)S(1)} %shared_gate.1.value_ref), custom_call_target="tpu_custom_call" | custom-call | flops 1073741824 | bytes 4194304 | tf_op jit(solution)/shard_map/shared_up/pallas_call | solution.py:292
  5.6 0.9 %copy-done.1 = bf16[512,4096]{1,0:T(8,128)(2,1)S(1)} copy-done((bf16[512,4096]{1,0:T(8,128)(2,1)S(1)}, bf16[512,4096]{1,0:T(8,128)(2,1)}, u32[]{:S(2)}) %copy-start.1) | copy-done | bytes 4194328
  6.5 0.0 copy-start.3
  6.5 0.7 %shared_first.1 = (bf16[1,256,1024]{2,1,0:T(8,128)(2,1)S(1)}, bf16[1,256,1024]{2,1,0:T(8,128)(2,1)S(1)}) custom-call(bf16[256,512]{1,0:T(8,128)(2,1)S(1)} %shared_up.1.hidden_ref, bf16[512,4096]{1,0:T(8,128)(2,1)S(1)} %copy-done.1), custom_call_target="tpu_custom_call" | custom-call | flops 536870912 | bytes 2097152 | tf_op jit(solution)/shard_map/shared_first/pallas_call | solution.py:301
  7.2 0.0 copy-start.2
  7.2 0.6 %collective-permute-start.4 = (bf16[1,256,1024]{2,1,0:T(8,128)(2,1)S(1)}, bf16[1,256,1024]{2,1,0:T(8,128)(2,1)S(1)}, u32[]{:S(2)}, u32[]{:S(2)}) collective-permute-start(bf16[1,256,1024]{2,1,0:T(8,128)(2,1)S(1)} %get-tuple-element.13), channel_id=1, source_target_pairs={{0,8},{8,0},{16,24},{24,16},{1,9},{9,1},{17,25},{25,17},{2,10},{10... | collective-permute-start | bytes 1572872 | tf_op jit(solution)/shard_map/ppermute | solution.py:313
  7.8 0.7 %shared_rest.1 = (bf16[256,1024]{1,0:T(8,128)(2,1)S(1)}, bf16[256,1024]{1,0:T(8,128)(2,1)S(1)}) custom-call(bf16[256,512]{1,0:T(8,128)(2,1)S(1)} %shared_up.1.hidden_ref, bf16[512,4096]{1,0:T(8,128)(2,1)S(1)} %copy-done.1), custom_call_target="tpu_custom_call" | custom-call | flops 536870912 | bytes 2097152 | tf_op jit(solution)/shard_map/shared_rest/pallas_call | solution.py:342
  8.5 0.1 collective-permute-start.6
  8.6 0.7 %collective-permute-done.4.a_ref = bf16[1,256,1024]{2,1,0:T(8,128)(2,1)S(1)} collective-permute-done((bf16[1,256,1024]{2,1,0:T(8,128)(2,1)S(1)}, bf16[1,256,1024]{2,1,0:T(8,128)(2,1)S(1)}, u32[]{:S(2)}, u32[]{:S(2)}) %collective-permute-start.4) | collective-permute-done | bytes 524320 | tf_op jit(solution)/shard_map/ppermute | solution.py:313
  9.3 0.1 add.1
  9.5 2.9 %collective-permute-start.5 = (bf16[256,1024]{1,0:T(8,128)(2,1)S(1)}, bf16[256,1024]{1,0:T(8,128)(2,1)S(1)}, u32[]{:S(2)}, u32[]{:S(2)}) collective-permute-start(bf16[256,1024]{1,0:T(8,128)(2,1)S(1)} %bitcast.3), channel_id=1, source_target_pairs={{0,16},{8,24},{16,0},{24,8},{1,17},{9,25},{17,1},{25,9},{2,18},{10... | collective-permute-start | bytes 1572872 | tf_op jit(solution)/shard_map/ppermute | solution.py:326
  12.4 1.5 %collective-permute-start = (bf16[3,2,4096]{2,1,0:T(2,128)(2,1)S(1)}, bf16[3,2,4096]{2,1,0:T(2,128)(2,1)S(1)}, u32[]{:S(2)}, u32[]{:S(2)}) collective-permute-start(bf16[3,2,4096]{2,1,0:T(2,128)(2,1)S(1)} %get-tuple-element.12), channel_id=1, source_target_pairs={{0,1},{1,0},{2,3},{3,2},{4,5},{5,4},{6,7},{7,6},{8,9},{9,8},{10,11... | collective-permute-start | bytes 147464 | tf_op jit(solution)/shard_map/ppermute | solution.py:269
  13.9 2.6 %collective-permute-done.refs_1_ = bf16[3,2,4096]{2,1,0:T(2,128)(2,1)S(1)} collective-permute-done((bf16[3,2,4096]{2,1,0:T(2,128)(2,1)S(1)}, bf16[3,2,4096]{2,1,0:T(2,128)(2,1)S(1)}, u32[]{:S(2)}, u32[]{:S(2)}) %collective-permute-start) | collective-permute-done | bytes 49184 | tf_op jit(solution)/shard_map/ppermute | solution.py:269
  16.5 2.6 %collective-permute-start.2 = (bf16[2,2,4096]{2,1,0:T(2,128)(2,1)S(1)}, bf16[2,2,4096]{2,1,0:T(2,128)(2,1)S(1)}, u32[]{:S(2)}, u32[]{:S(2)}) collective-permute-start(bf16[2,2,4096]{2,1,0:T(2,128)(2,1)S(1)} %pack.3), channel_id=1, source_target_pairs={{0,4},{1,5},{2,6},{3,7},{4,0},{5,1},{6,2},{7,3},{8,14},{9,15},{10,... | collective-permute-start | bytes 98312 | tf_op jit(solution)/shard_map/ppermute | solution.py:275
  19.1 0.0 copy-start.8
  19.1 1.6 %collective-permute-start.1 = (bf16[2,2,4096]{2,1,0:T(2,128)(2,1)S(1)}, bf16[2,2,4096]{2,1,0:T(2,128)(2,1)S(1)}, u32[]{:S(2)}, u32[]{:S(2)}) collective-permute-start(bf16[2,2,4096]{2,1,0:T(2,128)(2,1)S(1)} %pack.2), channel_id=1, source_target_pairs={{0,2},{1,3},{2,0},{3,1},{4,6},{5,7},{6,4},{7,5},{8,10},{9,11},{10,... | collective-permute-start | bytes 98312 | tf_op jit(solution)/shard_map/ppermute | solution.py:276
  20.6 0.6 %collective-permute-done.2.refs_3_ = bf16[2,2,4096]{2,1,0:T(2,128)(2,1)S(1)} collective-permute-done((bf16[2,2,4096]{2,1,0:T(2,128)(2,1)S(1)}, bf16[2,2,4096]{2,1,0:T(2,128)(2,1)S(1)}, u32[]{:S(2)}, u32[]{:S(2)}) %collective-permute-start.2) | collective-permute-done | bytes 32800 | tf_op jit(solution)/shard_map/ppermute | solution.py:275
  21.3 0.0 collective-permute-start.3
  21.3 1.7 %collective-permute-done.1.refs_2_ = bf16[2,2,4096]{2,1,0:T(2,128)(2,1)S(1)} collective-permute-done((bf16[2,2,4096]{2,1,0:T(2,128)(2,1)S(1)}, bf16[2,2,4096]{2,1,0:T(2,128)(2,1)S(1)}, u32[]{:S(2)}, u32[]{:S(2)}) %collective-permute-start.1) | collective-permute-done | bytes 32800 | tf_op jit(solution)/shard_map/ppermute | solution.py:276
  23.0 0.0 collective-permute-done.3.refs_4_
  23.0 0.0 copy-done.4
  23.0 0.0 copy-done.3
  23.0 0.0 copy-done.2
  23.0 2.5 %routed.1 = bf16[32,2,1024]{2,1,0:T(2,128)(2,1)} custom-call(bf16[3,2,4096]{2,1,0:T(2,128)(2,1)S(1)} %get-tuple-element.11.refs_0_.after_ref, bf16[3,2,4096]{2,1,0:T(2,128)(2,1)S(1)} %collective-permute-done.refs_1_, bf16[2,2,4096]{2,1,0:T(2,128)(2,1)S(1)} %collective-permute-done.1.refs_2_, bf16[2,2,4096]{2,1,0:T(2,128)(2,1)S(1)} %collective-permute-done.2.refs_3_, ...), custom_call_target="tpu_custom_call" | custom-call | flops 1073741824 | bytes 12582912 | tf_op jit(solution)/shard_map/routed/pallas_call | solution.py:328
  25.5 4.7 %all-to-all-start = ((bf16[32,2,1024]{2,1,0:T(2,128)(2,1)}), bf16[32,2,1024]{2,1,0:T(2,128)(2,1)S(1)}, u32[]{:S(2)}, u32[]{:S(2)}) async-start(bf16[32,2,1024]{2,1,0:T(2,128)(2,1)} %routed.1), calls=%async_computation | async-start | bytes 262144 | tf_op jit(solution)/shard_map/all_to_all | solution.py:338
  30.2 0.0 copy-done.8
  30.2 0.8 %mix.1.mix_ref = bf16[256,128]{1,0:T(8,128)(2,1)S(1)} custom-call(s32[8]{0:T(128)S(1)} %copy-done.9, s32[8]{0:T(128)S(1)} %copy-done.10, s32[8,256]{1,0:T(8,128)S(1)} %bitcast.5, f32[8,256]{1,0:T(8,128)S(1)} %bitcast.6), custom_call_target="tpu_custom_call" | custom-call | tf_op jit(solution)/shard_map/mix/pallas_call | solution.py:354
  31.0 0.0 collective-permute-done.6.refs_0_
  31.0 0.0 collective-permute-done.5.a_ref
  31.0 0.2 total.1.sum_ref
  31.2 6.8 %all-to-all-done.back_ref = bf16[32,2,1024]{2,1,0:T(2,128)(2,1)S(1)} async-done(((bf16[32,2,1024]{2,1,0:T(2,128)(2,1)}), bf16[32,2,1024]{2,1,0:T(2,128)(2,1)S(1)}, u32[]{:S(2)}, u32[]{:S(2)}) %all-to-all-start) | async-done | bytes 131104 | tf_op jit(solution)/shard_map/all_to_all | solution.py:338
  38.0 1.1 %combine.1 = bf16[256,1024]{1,0:T(8,128)(2,1)} custom-call(bf16[256,128]{1,0:T(8,128)(2,1)S(1)} %mix.1.mix_ref, bf16[32,2,1024]{2,1,0:T(2,128)(2,1)S(1)} %all-to-all-done.back_ref, f32[256,1024]{1,0:T(8,128)S(1)} %total.1.sum_ref), custom_call_target="tpu_custom_call" | custom-call | tf_op jit(solution)/shard_map/combine/pallas_call | solution.py:371
  (3 shorter events, 0.0 us)
Async XLA Ops:
  0.0 0.7 %copy-start.7 = (s32[256,8]{0,1:T(8,128)S(1)}, s32[256,8]{0,1:T(8,128)}, u32[]{:S(2)}) copy-start(s32[256,8]{0,1:T(8,128)} %param.12) | copy-start | bytes 24580
  0.0 0.7 %copy-start.9 = (s32[8]{0:T(128)S(1)}, s32[8]{0:T(128)}, u32[]{:S(2)}) copy-start(s32[8]{0:T(128)} %old_ref.3) | copy-start | bytes 100
  0.0 0.7 %copy-start.10 = (s32[8]{0:T(128)S(1)}, s32[8]{0:T(128)}, u32[]{:S(2)}) copy-start(s32[8]{0:T(128)} %new_ref.3) | copy-start | bytes 100
  0.0 1.6 %copy-start = (bf16[256,4096]{1,0:T(8,128)(2,1)S(1)}, bf16[256,4096]{1,0:T(8,128)(2,1)}, u32[]{:S(2)}) copy-start(bf16[256,4096]{1,0:T(8,128)(2,1)} %tok_ref.5) | copy-start | bytes 6291460
  0.0 2.9 %copy-start.6 = (bf16[4096,512]{1,0:T(8,128)(2,1)S(1)}, bf16[4096,512]{1,0:T(8,128)(2,1)}, u32[]{:S(2)}) copy-start(bf16[4096,512]{1,0:T(8,128)(2,1)} %gate_ref.1) | copy-start | bytes 12582916
  1.6 2.7 %copy-start.5 = (bf16[4096,512]{1,0:T(8,128)(2,1)S(1)}, bf16[4096,512]{1,0:T(8,128)(2,1)}, u32[]{:S(2)}) copy-start(bf16[4096,512]{1,0:T(8,128)(2,1)} %up_ref.1) | copy-start | bytes 12582916
  4.3 2.2 %copy-start.1 = (bf16[512,4096]{1,0:T(8,128)(2,1)S(1)}, bf16[512,4096]{1,0:T(8,128)(2,1)}, u32[]{:S(2)}) copy-start(bf16[512,4096]{1,0:T(8,128)(2,1)} %down_ref.3) | copy-start | bytes 12582916
  4.3 18.7 %copy-start.4 = (bf16[1,512,4096]{2,1,0:T(8,128)(2,1)S(1)}, bf16[1,512,4096]{2,1,0:T(8,128)(2,1)}, u32[]{:S(2)}) copy-start(bf16[1,512,4096]{2,1,0:T(8,128)(2,1)} %refs_7_.1) | copy-start | bytes 12582916
  6.5 16.5 %copy-start.3 = (bf16[1,4096,512]{2,1,0:T(8,128)(2,1)S(1)}, bf16[1,4096,512]{2,1,0:T(8,128)(2,1)}, u32[]{:S(2)}) copy-start(bf16[1,4096,512]{2,1,0:T(8,128)(2,1)} %refs_6_.1) | copy-start | bytes 12582916
  7.2 15.8 %copy-start.2 = (bf16[1,4096,512]{2,1,0:T(8,128)(2,1)S(1)}, bf16[1,4096,512]{2,1,0:T(8,128)(2,1)}, u32[]{:S(2)}) copy-start(bf16[1,4096,512]{2,1,0:T(8,128)(2,1)} %refs_5_.1) | copy-start | bytes 12582916
  7.2 2.1 %collective-permute-start.4 = (bf16[1,256,1024]{2,1,0:T(8,128)(2,1)S(1)}, bf16[1,256,1024]{2,1,0:T(8,128)(2,1)S(1)}, u32[]{:S(2)}, u32[]{:S(2)}) collective-permute-start(bf16[1,256,1024]{2,1,0:T(8,128)(2,1)S(1)} %get-tuple-element.13), channel_id=1, source_target_pairs={{0,8},{8,0},{16,24},{24,16},{1,9},{9,1},{17,25},{25,17},{2,10},{10... | collective-permute-start | bytes 1572872 | tf_op jit(solution)/shard_map/ppermute | solution.py:313
  8.5 22.5 %collective-permute-start.6 = (bf16[256,1024]{1,0:T(8,128)(2,1)S(1)}, bf16[256,1024]{1,0:T(8,128)(2,1)S(1)}, u32[]{:S(2)}, u32[]{:S(2)}) collective-permute-start(bf16[256,1024]{1,0:T(8,128)(2,1)S(1)} %get-tuple-element.16), channel_id=1, source_target_pairs={{0,8},{8,0},{16,24},{24,16},{1,9},{9,1},{17,25},{25,17},{2,10},{10... | collective-permute-start | bytes 1572872 | tf_op jit(solution)/shard_map/ppermute | solution.py:351
  9.5 21.5 %collective-permute-start.5 = (bf16[256,1024]{1,0:T(8,128)(2,1)S(1)}, bf16[256,1024]{1,0:T(8,128)(2,1)S(1)}, u32[]{:S(2)}, u32[]{:S(2)}) collective-permute-start(bf16[256,1024]{1,0:T(8,128)(2,1)S(1)} %bitcast.3), channel_id=1, source_target_pairs={{0,16},{8,24},{16,0},{24,8},{1,17},{9,25},{17,1},{25,9},{2,18},{10... | collective-permute-start | bytes 1572872 | tf_op jit(solution)/shard_map/ppermute | solution.py:326
  12.4 4.1 %collective-permute-start = (bf16[3,2,4096]{2,1,0:T(2,128)(2,1)S(1)}, bf16[3,2,4096]{2,1,0:T(2,128)(2,1)S(1)}, u32[]{:S(2)}, u32[]{:S(2)}) collective-permute-start(bf16[3,2,4096]{2,1,0:T(2,128)(2,1)S(1)} %get-tuple-element.12), channel_id=1, source_target_pairs={{0,1},{1,0},{2,3},{3,2},{4,5},{5,4},{6,7},{7,6},{8,9},{9,8},{10,11... | collective-permute-start | bytes 147464 | tf_op jit(solution)/shard_map/ppermute | solution.py:269
  16.5 4.8 %collective-permute-start.2 = (bf16[2,2,4096]{2,1,0:T(2,128)(2,1)S(1)}, bf16[2,2,4096]{2,1,0:T(2,128)(2,1)S(1)}, u32[]{:S(2)}, u32[]{:S(2)}) collective-permute-start(bf16[2,2,4096]{2,1,0:T(2,128)(2,1)S(1)} %pack.3), channel_id=1, source_target_pairs={{0,4},{1,5},{2,6},{3,7},{4,0},{5,1},{6,2},{7,3},{8,14},{9,15},{10,... | collective-permute-start | bytes 98312 | tf_op jit(solution)/shard_map/ppermute | solution.py:275
  19.1 11.1 %copy-start.8 = (f32[256,8]{0,1:T(8,128)S(1)}, f32[256,8]{0,1:T(8,128)}, u32[]{:S(2)}) copy-start(f32[256,8]{0,1:T(8,128)} %param.13) | copy-start | bytes 24580
  19.1 3.9 %collective-permute-start.1 = (bf16[2,2,4096]{2,1,0:T(2,128)(2,1)S(1)}, bf16[2,2,4096]{2,1,0:T(2,128)(2,1)S(1)}, u32[]{:S(2)}, u32[]{:S(2)}) collective-permute-start(bf16[2,2,4096]{2,1,0:T(2,128)(2,1)S(1)} %pack.2), channel_id=1, source_target_pairs={{0,2},{1,3},{2,0},{3,1},{4,6},{5,7},{6,4},{7,5},{8,10},{9,11},{10,... | collective-permute-start | bytes 98312 | tf_op jit(solution)/shard_map/ppermute | solution.py:276
  21.3 1.7 %collective-permute-start.3 = (bf16[2,2,4096]{2,1,0:T(2,128)(2,1)S(1)}, bf16[2,2,4096]{2,1,0:T(2,128)(2,1)S(1)}, u32[]{:S(2)}, u32[]{:S(2)}) collective-permute-start(bf16[2,2,4096]{2,1,0:T(2,128)(2,1)S(1)} %collective-permute-done.2.refs_3_), channel_id=1, source_target_pairs={{0,8},{8,0},{16,24},{24,16},{1,9},{9,1},{17,25},{25,17},{2,10},{10... | collective-permute-start | bytes 98312 | tf_op jit(solution)/shard_map/ppermute | solution.py:277
  25.5 12.5 %all-to-all-start = ((bf16[32,2,1024]{2,1,0:T(2,128)(2,1)}), bf16[32,2,1024]{2,1,0:T(2,128)(2,1)S(1)}, u32[]{:S(2)}, u32[]{:S(2)}) async-start(bf16[32,2,1024]{2,1,0:T(2,128)(2,1)} %routed.1), calls=%async_computation | async-start | bytes 262144 | tf_op jit(solution)/shard_map/all_to_all | solution.py:338
